TPU v7x, 256 devices: a whole 4x4x8 slice. The times are simulated.
256 devices in a mesh: grp: 32 (over z, x_lo, core), freq: 8 (over x_hi, y).
Axes of the slice: x: 4 (x_hi: 2, x_lo: 2; x = x_hi * 2 + x_lo), y: 4, z: 8, core: 2. Of those that a mesh axis runs over, the one named last changes fastest.
Arguments:
- spectra: bfloat16 [8, 8192, 1024], P('freq', 'grp'), may hold values from -3000 to 3000
- valid: int32 [8192, 512], P('grp'), may hold values 0 or 1
- station_index: int32 [16], replicated, may hold values from 0 to 8191, as said below
Outputs:
- cross: bfloat16 [8, 2, 8192, 8192], P('freq', None, 'grp')
- station_gather: float32 [16, 8192, 256], P(None, 'grp', 'freq')
Inputs may be any that keep to these rules, and one draw needn't show every extreme that they name: `station_index`: 16 distinct channel numbers.
All inputs are finite; a program needn't handle non-finite values. No bound on the sum of `valid` on one device may be relied on, other than what follows from the above.
Results may differ from a plain program's by a relative error of at most 0.0056.
Values may be sent and summed in bfloat16 or wider, within the bound.
A program may use at most 128 MiB of HBM per device.

v0:
```python
import math

import jax
import jax.numpy as jnp
from jax import lax
from jax.sharding import PartitionSpec as P

LAGS = 256


def on_device(spectra, valid, station_index):
    bin_count, chan_count, double_width = spectra.shape
    window_count = double_width // 2
    group_index = lax.axis_index("grp")
    spectrum_f32 = spectra.astype(jnp.float32)
    real_part = spectrum_f32[..., :window_count]
    imag_part = spectrum_f32[..., window_count:]
    local_power = jnp.sum(real_part * real_part + imag_part * imag_part, axis=0)
    band_power = lax.psum(local_power, "freq")
    total_bins = bin_count * lax.axis_size("freq")
    factor = lax.rsqrt(band_power / total_bins + 1e-05) * valid.astype(jnp.float32)
    whitened = (spectrum_f32 * jnp.concatenate([factor, factor], axis=1)[None]).astype(jnp.bfloat16)
    swapped = jnp.concatenate([whitened[..., window_count:], -whitened[..., :window_count]], axis=2)
    stacked = jnp.concatenate([whitened, swapped], axis=1)
    scaling = 1.0 / math.sqrt(window_count)
    peer_rows = lax.all_gather(whitened, "grp", axis=1, tiled=True)
    product = jnp.einsum("bkw,bjw->bkj", stacked, peer_rows, preferred_element_type=jnp.float32)
    cross = (
        (product * scaling)
        .astype(jnp.bfloat16)
        .reshape(bin_count, 2, chan_count, peer_rows.shape[1])
    )
    station_count = station_index.shape[0]
    local_rel = station_index - group_index * chan_count
    selector = (local_rel[:, None] == jnp.arange(chan_count, dtype=jnp.int32)[None, :]).astype(
        jnp.bfloat16
    )
    picked = jnp.einsum("sc,bcw->bsw", selector, whitened, preferred_element_type=jnp.float32)
    station_rows = lax.psum(picked.astype(jnp.bfloat16), "grp")
    station_swapped = jnp.concatenate(
        [station_rows[..., window_count:], -station_rows[..., :window_count]], axis=2
    )
    station_left = jnp.concatenate([station_rows, station_swapped], axis=1)
    kernel = (
        jnp.einsum("bkw,bjw->bkj", station_left, whitened, preferred_element_type=jnp.float32)
        * scaling
    )
    kernel = kernel.reshape(bin_count, 2, station_count, chan_count)
    freq_index = lax.axis_index("freq")
    bin_values = (freq_index * bin_count + jnp.arange(bin_count, dtype=jnp.int32)).astype(
        jnp.float32
    ) + 1.0
    lag_values = jnp.arange(LAGS).astype(jnp.float32)
    phase = math.pi * bin_values[:, None] * lag_values[None, :] / LAGS
    lag_table = jnp.stack([jnp.cos(phase), -jnp.sin(phase)], axis=1)
    partial_lags = jnp.einsum(
        "frsc,frl->scl", kernel, lag_table, precision=lax.Precision.HIGHEST
    ) / math.sqrt(total_bins)
    station_gather = lax.psum_scatter(partial_lags, "freq", scatter_dimension=2, tiled=True)
    return (cross, station_gather)


def solution(mesh):
    placed = (P("freq", "grp", None), P("grp", None), P())
    return jax.shard_map(
        on_device,
        mesh=mesh,
        in_specs=placed,
        out_specs=(P("freq", None, "grp", None), P(None, "grp", "freq")),
        check_vma=False,
    )
```

profile of v0, /device:TPU:1, one launch (start us, length us, event | category | flops | bytes accessed | tf_op | source)
XLA Modules:
  0.0 317.3 jit_solution(2956851506514024311)
XLA Ops:
  7.2 0.0 all-reduce.2.cloned.1.call-start
  7.2 1.1 convert_element_type.43
  8.4 0.9 fusion.12
  9.3 0.0 all-reduce.2.cloned.1.call-update
  9.3 0.0 all-gather.2.cloned.1.call-start
  9.3 90.7 %all-reduce.2.cloned.1.call-done = f32[256,512]{1,0:T(8,128)} async-done(((f32[256,512]{1,0:T(8,128)}), f32[256,512]{1,0:T(8,128)}) %all-reduce.2.cloned.1.call-update) | async-done | bytes 524304 | tf_op jit(solution)/shard_map/psum | solution.py:19
  100.0 1.3 convert_multiply_fusion
  101.3 2.0 fusion.6
  103.3 0.0 copy-start
  103.3 0.0 all-gather.2.cloned.1.call-update
  103.3 0.0 reduce-scatter.2.cloned.1.call-start
  103.4 0.1 sine_negate_fusion
  103.5 0.7 broadcast_subtract_fusion
  104.1 1.3 fusion.4
  105.4 108.8 %psum.15 = bf16[1,16,1024]{2,1,0:T(8,128)(2,1)S(1)} all-reduce(bf16[1,16,1024]{2,1,0:T(8,128)(2,1)S(1)} %fusion.4), channel_id=1, replica_groups=mesh['grp'=32,'freq'=8] {'grp'}, use_global_device_ids=true, to_apply=%region_1.0 | all-reduce | flops 16384 | bytes 65536 | tf_op jit(solution)/shard_map/psum | solution.py:39
  214.2 1.3 convolution_multiply_fusion.1
  215.5 5.1 %convolution_multiply_fusion = f32[16,256,256]{1,2,0:T(8,128)} fusion(f32[2,16,256]{2,1,0:T(8,128)S(1)} %bitcast.34, f32[1,1,256]{2,1,0:T(1,128)S(1)} %get-tuple-element.6, f32[1,1,256]{2,1,0:T(1,128)S(1)} %get-tuple-element.7), kind=kOutput, calls=%fused_computation.3 | convolution fusion | flops 26214912 | bytes 4229120 | tf_op jit(solution)/shard_map/frsc,frl->scl/dot_general | solution.py:56
  220.6 0.0 reduce-scatter.2.cloned.1.call-update
  220.6 0.0 copy-done
  220.7 0.0 all-gather.2.cloned.1.call-done
  220.7 25.8 %multiply_convert_fusion = bf16[512,8192]{1,0:T(8,128)(2,1)} fusion(bf16[1,8192,1024]{2,1,0:T(8,128)(2,1)} %all-gather.2.cloned.1.call-done, bf16[1,256,512]{2,1,0:T(8,128)(2,1)S(1)} %get-tuple-element.3, bf16[1,256,512]{2,1,0:T(8,128)(2,1)S(1)} %get-tuple-element.2, bf16[1,256,1024]{2,1,0:T(8,128)(2,1)S(1)} %copy-done), kind=kOutput, calls=%fused_computation.2 | convolution fusion | flops 8601468928 | bytes 26214400 | tf_op jit(solution)/shard_map/bkw,bjw->bkj/dot_general | solution.py:27
  246.5 64.3 %reduce-scatter.2.cloned.1.call-done = f32[16,256,32]{1,2,0:T(8,128)} async-done(((f32[16,256,256]{1,2,0:T(8,128)}), f32[16,256,32]{1,2,0:T(8,128)}) %reduce-scatter.2.cloned.1.call-update) | async-done | bytes 524304 | tf_op jit(solution)/shard_map/reduce_scatter | solution.py:59
  (2 shorter events, 0.0 us)
Async XLA Ops:
  7.2 92.9 %all-reduce.2.cloned.1.call-start = ((), (), s32[]{:S(2)}) async-start(), calls=%async_computation.1 | async-start | bytes 1048576 | tf_op jit(solution)/shard_map/psum | solution.py:19
  9.3 211.4 %all-gather.2.cloned.1.call-start = ((), (), s32[]{:S(2)}) async-start(), calls=%async_computation.2 | async-start | bytes 17301504 | tf_op jit(solution)/shard_map/all_gather | solution.py:26
  103.3 117.3 %copy-start = (bf16[1,256,1024]{2,1,0:T(8,128)(2,1)S(1)}, bf16[1,256,1024]{2,1,0:T(8,128)(2,1)}, u32[]{:S(2)}) copy-start(bf16[1,256,1024]{2,1,0:T(8,128)(2,1)} %fusion.6) | copy-start | bytes 1572868
  103.3 207.4 %reduce-scatter.2.cloned.1.call-start = ((), (), s32[]{:S(2)}) async-start(), calls=%async_computation.3 | async-start | bytes 4718592 | tf_op jit(solution)/shard_map/reduce_scatter | solution.py:59
Sparse Core Ops, SparseCore 0:
  11.2 88.7 all-reduce.1
  103.5 105.8 all-gather.1
  220.7 89.9 reduce-scatter.1
where the time goes:
time: 318 us; the launch traced here: 317 us
  waiting for transfers between devices  155 us (49%)
  blocking collectives  109 us (34%)
  matrix products  33.4 us (11%)
  between operations  13.8 us (4%)
  other arithmetic  6.11 us (2%)
    psum x1, blocking collectives, on_device(): station_rows = lax.psum(picked.astype(jnp.bfloat16), 'grp')  109 us
    psum x1, waiting for transfers between devices, on_device(): band_power = lax.psum(local_power, 'freq')  90.7 us
    reduce_scatter x1, waiting for transfers between devices, on_device(): lax.psum_scatter(partial_lags, 'freq', scatter_dimension=2, tiled=True)  64.3 us
    dot_general x1, matrix products, on_device(): jnp.einsum('bkw,bjw->bkj', stacked, peer_rows, preferred_element_type=jnp...  25.8 us
  transfers between devices with their start and end apart: 3, of which 2 were waited for; matrix products, arithmetic and copies ran while one was open for 11% of the time, Pallas kernels for 0%

commit v1 on v0

v1 whole, which is shorter than its diff:
```python
import math

import jax
import jax.numpy as jnp
from jax import lax
from jax.sharding import Mesh
from jax.sharding import PartitionSpec as P

LAGS = 256
GRP = ("chip", "core")


def on_device(spectra, valid, station_index):
    bin_count, chan_count, double_width = spectra.shape
    window_count = double_width // 2
    spectrum_f32 = spectra.astype(jnp.float32)
    real_part = spectrum_f32[..., :window_count]
    imag_part = spectrum_f32[..., window_count:]
    local_power = jnp.sum(real_part * real_part + imag_part * imag_part, axis=0)
    band_power = lax.psum(local_power, "freq")
    freq_count = lax.axis_size("freq")
    total_bins = bin_count * freq_count
    factor = lax.rsqrt(band_power / total_bins + 1e-05) * valid.astype(jnp.float32)
    whitened = (spectrum_f32 * jnp.concatenate([factor, factor], axis=1)[None]).astype(jnp.bfloat16)
    swapped = jnp.concatenate([whitened[..., window_count:], -whitened[..., :window_count]], axis=2)
    stacked = jnp.concatenate([whitened, swapped], axis=1)
    scaling = 1.0 / math.sqrt(window_count)

    chip_count = lax.axis_size("chip")
    core_count = lax.axis_size("core")
    same_core = lax.all_gather(whitened, "chip", axis=1)
    both_cores = lax.all_gather(same_core, "core", axis=2)
    peer_rows = both_cores.reshape(bin_count, chip_count * core_count * chan_count, double_width)

    product = jnp.einsum("bkw,bjw->bkj", stacked, peer_rows, preferred_element_type=jnp.float32)
    cross = (
        (product * scaling)
        .astype(jnp.bfloat16)
        .reshape(bin_count, 2, chan_count, peer_rows.shape[1])
    )

    station_count = station_index.shape[0]
    station_rows = jnp.take(peer_rows, station_index, axis=1)
    station_swapped = jnp.concatenate(
        [station_rows[..., window_count:], -station_rows[..., :window_count]], axis=2
    )
    station_left = jnp.concatenate([station_rows, station_swapped], axis=1)
    kernel = (
        jnp.einsum("bkw,bjw->bkj", station_left, whitened, preferred_element_type=jnp.float32)
        * scaling
    )
    kernel = kernel.reshape(bin_count, 2, station_count, chan_count)
    all_bins = lax.all_gather(kernel, "freq", axis=0, tiled=True)

    lag_share = LAGS // freq_count
    freq_index = lax.axis_index("freq")
    bin_values = jnp.arange(total_bins, dtype=jnp.float32) + 1.0
    lag_values = (freq_index * lag_share + jnp.arange(lag_share, dtype=jnp.int32)).astype(jnp.float32)
    phase = math.pi * bin_values[:, None] * lag_values[None, :] / LAGS
    lag_table = jnp.stack([jnp.cos(phase), -jnp.sin(phase)], axis=1)
    station_gather = jnp.einsum(
        "frsc,frl->scl", all_bins, lag_table, precision=lax.Precision.HIGHEST
    ) / math.sqrt(total_bins)
    return (cross, station_gather)


def solution(mesh):
    grp_size, freq_size = mesh.devices.shape
    fine = Mesh(mesh.devices.reshape(grp_size // 2, 2, freq_size), ("chip", "core", "freq"))
    placed = (P("freq", GRP, None), P(GRP, None), P())
    return jax.shard_map(
        on_device,
        mesh=fine,
        in_specs=placed,
        out_specs=(P("freq", None, GRP, None), P(None, GRP, "freq")),
        check_vma=False,
    )
```

time: 318 us -> 395 us (1.24); the launches traced: 317 us -> 390 us
  waiting for transfers between devices: 155 us -> 314 us
  blocking collectives: 109 us -> 28.6 us
  matrix products: 33.4 us -> 17.3 us
  local copies, waits for them, and re-layouts: 0.01 us -> 8.53 us
    all_gather x1 -> x2, waiting for transfers between devices: 0.02 us -> 223 us  [the longest x1 186 us: on_device(): same_core = lax.all_gather(whitened, 'chip', axis=1)]
    psum x1 -> x0, blocking collectives: 109 us -> none  [on_device(): station_rows = lax.psum(picked.astype(jnp.bfloat16), 'grp')]
    reduce_scatter x1 -> x0, waiting for transfers between devices: 64.3 us -> none  [on_device(): lax.psum_scatter(partial_lags, 'freq', scatter_dimension=2, tiled=True)]
    all_gather x0 -> x1, blocking collectives: none -> 28.6 us  [on_device(): all_bins = lax.all_gather(kernel, 'freq', axis=0, tiled=True)]
    dot_general x1, matrix products: 25.8 us -> 14.5 us  [on_device(): jnp.einsum('bkw,bjw->bkj', stacked, peer_rows, preferred_element_type=jnp...]
    gather x0 -> x1, local copies, waits for them, and re-layouts: none -> 8.53 us  [on_device(): station_rows = jnp.take(peer_rows, station_index, axis=1)]
    dot_general x2 -> x1, matrix products: 6.37 us -> 1.49 us  [on_device(): jnp.einsum('frsc,frl->scl', all_bins, lag_table, precision=lax.Precision....]
  transfers between devices with their start and end apart: 3 -> 3, of which waited for: 2 -> 3; matrix products, arithmetic and copies ran while one was open for 11% -> 1% of each run, Pallas kernels for 0% -> 0%
where the time goes in v1:
time: 395 us; the launch traced here: 390 us
  waiting for transfers between devices  314 us (79%)
  blocking collectives  28.6 us (7%)
  matrix products  17.3 us (4%)
  between operations  13.8 us (3%)
  local copies, waits for them, and re-layouts  8.53 us (2%)
  other arithmetic  7.93 us (2%)
    all_gather x1, waiting for transfers between devices, on_device(): same_core = lax.all_gather(whitened, 'chip', axis=1)  186 us
    psum x1, waiting for transfers between devices, on_device(): band_power = lax.psum(local_power, 'freq')  90.7 us
    all_gather x1, waiting for transfers between devices, on_device(): both_cores = lax.all_gather(same_core, 'core', axis=2)  36.8 us
    all_gather x1, blocking collectives, on_device(): all_bins = lax.all_gather(kernel, 'freq', axis=0, tiled=True)  28.6 us
    dot_general x1, matrix products, on_device(): jnp.einsum('bkw,bjw->bkj', stacked, peer_rows, preferred_element_type=jnp...  14.5 us
    gather x1, local copies, waits for them, and re-layouts, on_device(): station_rows = jnp.take(peer_rows, station_index, axis=1)  8.53 us
  transfers between devices with their start and end apart: 3, of which 3 were waited for; matrix products, arithmetic and copies ran while one was open for 1% of the time, Pallas kernels for 0%

profile of v1, /device:TPU:1, one launch (start us, length us, event | category | flops | bytes accessed | tf_op | source)
XLA Modules:
  0.0 389.9 jit_solution(18342799320419296325)
XLA Ops:
  7.2 0.0 all-reduce.2.cloned.1.call-start
  7.2 1.1 convert_element_type.20
  8.4 0.9 fusion.8
  9.3 0.0 all-reduce.2.cloned.1.call-update
  9.3 0.0 all-gather.5.cloned.1.call-start
  9.3 90.7 %all-reduce.2.cloned.1.call-done = f32[256,512]{1,0:T(8,128)} async-done(((f32[256,512]{1,0:T(8,128)}), f32[256,512]{1,0:T(8,128)}) %all-reduce.2.cloned.1.call-update) | async-done | bytes 524304 | tf_op jit(solution)/shard_map/psum | solution.py:20
  100.0 1.3 convert_multiply_fusion
  101.3 2.0 fusion.2
  103.3 0.0 all-gather.5.cloned.1.call-update
  103.3 0.0 all-gather.7.cloned.1.call-start
  103.4 186.1 %all-gather.5.cloned.1.call-done = bf16[16,256,1024]{2,1,0:T(8,128)(2,1)} async-done(((bf16[1,256,1024]{2,1,0:T(8,128)(2,1)}), bf16[16,256,1024]{2,1,0:T(8,128)(2,1)}) %all-gather.5.cloned.1.call-update) | async-done | bytes 8388624 | tf_op jit(solution)/shard_map/all_gather | solution.py:31
  289.5 0.0 all-gather.7.cloned.1.call-update
  289.5 0.7 compare_select_fusion
  290.2 0.7 compare_and_fusion
  290.9 0.1 fusion.17
  291.0 1.1 fusion.21
  292.0 36.8 %all-gather.7.cloned.1.call-done = bf16[16,512,1024]{2,1,0:T(8,128)(2,1)} async-done(((bf16[16,256,1024]{2,1,0:T(8,128)(2,1)}), bf16[16,512,1024]{2,1,0:T(8,128)(2,1)}) %all-gather.7.cloned.1.call-update) | async-done | bytes 16777232 | tf_op jit(solution)/shard_map/all_gather | solution.py:32
  328.8 8.5 %gather_fusion = bf16[16,1024]{1,0:T(8,128)(2,1)S(1)} fusion(bf16[8192,1024]{1,0:T(8,128)(2,1)} %bitcast.32, s32[1024]{0:T(1024)S(1)} %pad_clamp_fusion), kind=kCustom, calls=%fused_computation | custom fusion | bytes 65600 | tf_op jit(solution)/shard_map/jit(_take)/gather | solution.py:43
  337.4 0.1 bitcast_select_fusion
  337.4 1.3 convolution_multiply_fusion
  338.8 28.6 %all_gather.19 = f32[8,2,16,256]{3,2,1,0:T(8,128)S(1)} all-gather(f32[1,2,16,256]{3,2,1,0:T(8,128)S(1)} %bitcast.31), channel_id=1, replica_groups=mesh['chip'=16,'core'=2,'freq'=8] {'freq'}, dimensions={0}, use_global_device_ids=true | all-gather | bytes 294912 | tf_op jit(solution)/shard_map/all_gather | solution.py:53
  367.3 14.5 %multiply_convert_fusion = bf16[512,8192]{1,0:T(8,128)(2,1)} fusion(bf16[8192,1024]{1,0:T(8,128)(2,1)} %bitcast.33, bf16[1,256,512]{2,1,0:T(8,128)(2,1)S(1)} %get-tuple-element.3, bf16[1,256,512]{2,1,0:T(8,128)(2,1)S(1)} %get-tuple-element.2, bf16[1,256,1024]{2,1,0:T(8,128)(2,1)} %fusion.2), kind=kOutput, calls=%fused_computation.1 | convolution fusion | flops 8601468928 | bytes 26214400 | tf_op jit(solution)/shard_map/bkw,bjw->bkj/dot_general | solution.py:35
  381.9 1.5 fusion
  (4 shorter events, 0.0 us)
Async XLA Ops:
  7.2 92.9 %all-reduce.2.cloned.1.call-start = ((), (), s32[]{:S(2)}) async-start(), calls=%async_computation | async-start | bytes 1048576 | tf_op jit(solution)/shard_map/psum | solution.py:20
  9.3 280.2 %all-gather.5.cloned.1.call-start = ((), (), s32[]{:S(2)}) async-start(), calls=%async_computation.1 | async-start | bytes 8912896 | tf_op jit(solution)/shard_map/all_gather | solution.py:31
  103.3 225.5 %all-gather.7.cloned.1.call-start = ((), (), s32[]{:S(2)}) async-start(), calls=%async_computation.2 | async-start | bytes 25165824 | tf_op jit(solution)/shard_map/all_gather | solution.py:32
Sparse Core Ops, SparseCore 0:
  11.2 88.7 all-reduce.1
  103.4 185.9 all-gather.4
  291.4 37.3 all-gather.6

commit v2 on v1

v2 whole, which is shorter than its diff:
```python
import functools
import math

import jax
import jax.numpy as jnp
from jax import lax
from jax.experimental import pallas as pl
from jax.experimental.pallas import tpu as pltpu
from jax.sharding import PartitionSpec as P

LAGS = 256
MESH = pl.DeviceIdType.MESH


def _greet(peers, here):
    barrier = pltpu.get_barrier_semaphore()
    for k in range(1, peers):
        pl.semaphore_signal(barrier, inc=1, device_id=here((lax.axis_index("freq") + k) % peers), device_id_type=MESH)
    pl.semaphore_wait(barrier, peers - 1)


def _psum_kernel(peers, x_ref, out_ref, parts, send_a, recv_a, send_b, recv_b):
    me = lax.axis_index("freq")
    grp = lax.axis_index("grp")
    rows = x_ref.shape[0] // peers

    def here(peer):
        return (grp, peer)

    _greet(peers, here)
    scatter = []
    for k in range(1, peers):
        peer = (me + k) % peers
        copy = pltpu.make_async_remote_copy(
            src_ref=x_ref.at[pl.ds(pl.multiple_of(peer * rows, rows), rows)],
            dst_ref=parts.at[me],
            send_sem=send_a.at[peer],
            recv_sem=recv_a.at[me],
            device_id=here(peer),
            device_id_type=MESH,
        )
        copy.start()
        scatter.append(copy)
    own = x_ref[pl.ds(pl.multiple_of(me * rows, rows), rows), :]
    for k in range(1, peers):
        src = (me + peers - k) % peers
        pltpu.make_async_remote_copy(
            src_ref=x_ref.at[pl.ds(0, rows)],
            dst_ref=parts.at[src],
            send_sem=send_a.at[src],
            recv_sem=recv_a.at[src],
            device_id=here(src),
            device_id_type=MESH,
        ).wait_recv()
    for copy in scatter:
        copy.wait_send()
    parts[me] = own
    total = parts[0]
    for src in range(1, peers):
        total = total + parts[src]
    out_ref[pl.ds(pl.multiple_of(me * rows, rows), rows), :] = total
    gather = []
    for k in range(1, peers):
        peer = (me + k) % peers
        copy = pltpu.make_async_remote_copy(
            src_ref=out_ref.at[pl.ds(pl.multiple_of(me * rows, rows), rows)],
            dst_ref=out_ref.at[pl.ds(pl.multiple_of(me * rows, rows), rows)],
            send_sem=send_b.at[peer],
            recv_sem=recv_b.at[me],
            device_id=here(peer),
            device_id_type=MESH,
        )
        copy.start()
        gather.append(copy)
    for k in range(1, peers):
        src = (me + peers - k) % peers
        pltpu.make_async_remote_copy(
            src_ref=out_ref.at[pl.ds(pl.multiple_of(src * rows, rows), rows)],
            dst_ref=out_ref.at[pl.ds(pl.multiple_of(src * rows, rows), rows)],
            send_sem=send_b.at[src],
            recv_sem=recv_b.at[src],
            device_id=here(src),
            device_id_type=MESH,
        ).wait_recv()
    for copy in gather:
        copy.wait_send()


def freq_psum(x, peers):
    rows, cols = x.shape
    return pl.pallas_call(
        functools.partial(_psum_kernel, peers),
        out_shape=jax.ShapeDtypeStruct((rows, cols), x.dtype),
        in_specs=[pl.BlockSpec(memory_space=pltpu.VMEM)],
        out_specs=pl.BlockSpec(memory_space=pltpu.VMEM),
        scratch_shapes=[
            pltpu.VMEM((peers, rows // peers, cols), x.dtype),
            pltpu.SemaphoreType.DMA((peers,)),
            pltpu.SemaphoreType.DMA((peers,)),
            pltpu.SemaphoreType.DMA((peers,)),
            pltpu.SemaphoreType.DMA((peers,)),
        ],
        compiler_params=pltpu.CompilerParams(collective_id=0, has_side_effects=True),
    )(x)


def _gather_kernel(peers, x_ref, out_ref, send_sem, recv_sem):
    me = lax.axis_index("freq")
    grp = lax.axis_index("grp")

    def here(peer):
        return (grp, peer)

    _greet(peers, here)
    sent = []
    for k in range(1, peers):
        peer = (me + k) % peers
        copy = pltpu.make_async_remote_copy(
            src_ref=x_ref,
            dst_ref=out_ref.at[me],
            send_sem=send_sem.at[peer],
            recv_sem=recv_sem.at[me],
            device_id=here(peer),
            device_id_type=MESH,
        )
        copy.start()
        sent.append(copy)
    out_ref[me] = x_ref[...]
    for k in range(1, peers):
        src = (me + peers - k) % peers
        pltpu.make_async_remote_copy(
            src_ref=x_ref,
            dst_ref=out_ref.at[src],
            send_sem=send_sem.at[src],
            recv_sem=recv_sem.at[src],
            device_id=here(src),
            device_id_type=MESH,
        ).wait_recv()
    for copy in sent:
        copy.wait_send()


def freq_gather(x, peers):
    return pl.pallas_call(
        functools.partial(_gather_kernel, peers),
        out_shape=jax.ShapeDtypeStruct((peers, *x.shape), x.dtype),
        in_specs=[pl.BlockSpec(memory_space=pltpu.VMEM)],
        out_specs=pl.BlockSpec(memory_space=pltpu.VMEM),
        scratch_shapes=[
            pltpu.SemaphoreType.DMA((peers,)),
            pltpu.SemaphoreType.DMA((peers,)),
        ],
        compiler_params=pltpu.CompilerParams(collective_id=1, has_side_effects=True),
    )(x)


def on_device(spectra, valid, station_index):
    bin_count, chan_count, double_width = spectra.shape
    window_count = double_width // 2
    freq_count = lax.axis_size("freq")
    spectrum_f32 = spectra.astype(jnp.float32)
    real_part = spectrum_f32[..., :window_count]
    imag_part = spectrum_f32[..., window_count:]
    local_power = jnp.sum(real_part * real_part + imag_part * imag_part, axis=0)
    band_power = freq_psum(local_power, freq_count)
    total_bins = bin_count * freq_count
    factor = lax.rsqrt(band_power / total_bins + 1e-05) * valid.astype(jnp.float32)
    whitened = (spectrum_f32 * jnp.concatenate([factor, factor], axis=1)[None]).astype(jnp.bfloat16)
    swapped = jnp.concatenate([whitened[..., window_count:], -whitened[..., :window_count]], axis=2)
    stacked = jnp.concatenate([whitened, swapped], axis=1)
    scaling = 1.0 / math.sqrt(window_count)
    peer_rows = lax.all_gather(whitened, "grp", axis=1, tiled=True)
    product = jnp.einsum("bkw,bjw->bkj", stacked, peer_rows, preferred_element_type=jnp.float32)
    cross = (
        (product * scaling)
        .astype(jnp.bfloat16)
        .reshape(bin_count, 2, chan_count, peer_rows.shape[1])
    )

    station_count = station_index.shape[0]
    station_rows = jnp.take(peer_rows, station_index, axis=1, mode="clip")
    station_swapped = jnp.concatenate(
        [station_rows[..., window_count:], -station_rows[..., :window_count]], axis=2
    )
    station_left = jnp.concatenate([station_rows, station_swapped], axis=1)
    kernel = (
        jnp.einsum("bkw,bjw->bkj", station_left, whitened, preferred_element_type=jnp.float32)
        * scaling
    )
    kernel = kernel.reshape(2, station_count, chan_count)
    all_bins = freq_gather(kernel, freq_count)

    lag_share = LAGS // freq_count
    freq_index = lax.axis_index("freq")
    bin_values = jnp.arange(total_bins, dtype=jnp.float32) + 1.0
    lag_values = (freq_index * lag_share + jnp.arange(lag_share, dtype=jnp.int32)).astype(jnp.float32)
    phase = math.pi * bin_values[:, None] * lag_values[None, :] / LAGS
    lag_table = jnp.stack([jnp.cos(phase), -jnp.sin(phase)], axis=1)
    station_gather = jnp.einsum(
        "frsc,frl->scl", all_bins, lag_table, precision=lax.Precision.HIGHEST
    ) / math.sqrt(total_bins)
    return (cross, station_gather)


def solution(mesh):
    placed = (P("freq", "grp", None), P("grp", None), P())
    return jax.shard_map(
        on_device,
        mesh=mesh,
        in_specs=placed,
        out_specs=(P("freq", None, "grp", None), P(None, "grp", "freq")),
        check_vma=False,
    )
```

time: 395 us -> 184 us (0.47); the launches traced: 390 us -> 184 us
  waiting for transfers between devices: 314 us -> 102 us
  Pallas kernels: 0 us -> 33.1 us
  blocking collectives: 28.6 us -> 0 us
    all_gather x2 -> x1, waiting for transfers between devices: 223 us -> 102 us  [on_device(): peer_rows = lax.all_gather(whitened, 'grp', axis=1, tiled=True)]
    psum x1 -> x0, waiting for transfers between devices: 90.7 us -> none  [on_device(): band_power = lax.psum(local_power, 'freq')]
    pallas_call x0 -> x2, Pallas kernels: none -> 33.1 us  [the longest x1 21.5 us: freq_psum(): pl.pallas_call(functools.partial(_psum_kernel, peers), out_shape=jax.Shap...]
    all_gather x1 -> x0, blocking collectives: 28.6 us -> none  [on_device(): all_bins = lax.all_gather(kernel, 'freq', axis=0, tiled=True)]
  transfers between devices with their start and end apart: 3 -> 1, of which waited for: 3 -> 1; matrix products, arithmetic and copies ran while one was open for 1% -> 1% of each run, Pallas kernels for 0% -> 0%
where the time goes in v2:
time: 184 us
  waiting for transfers between devices  102 us (55%)
  Pallas kernels  33.1 us (18%)
  matrix products  18.9 us (10%)
  between operations  14.1 us (8%)
  local copies, waits for them, and re-layouts  8.53 us (5%)
  other arithmetic  7.19 us (4%)
    all_gather x1, waiting for transfers between devices, on_device(): peer_rows = lax.all_gather(whitened, 'grp', axis=1, tiled=True)  102 us
    pallas_call x1, Pallas kernels, freq_psum(): pl.pallas_call(functools.partial(_psum_kernel, peers), out_shape=jax.Shap...  21.5 us
    dot_general x1, matrix products, on_device(): jnp.einsum('bkw,bjw->bkj', stacked, peer_rows, preferred_element_type=jnp...  14.5 us
    pallas_call x1, Pallas kernels, freq_gather(): pl.pallas_call(functools.partial(_gather_kernel, peers), out_shape=jax.Sh...  11.6 us
    gather x1, local copies, waits for them, and re-layouts, on_device(): station_rows = jnp.take(peer_rows, station_index, axis=1, mode='clip')  8.53 us
  transfers between devices with their start and end apart: 1, of which 1 were waited for; matrix products, arithmetic and copies ran while one was open for 1% of the time, Pallas kernels for 0%

profile of v2, /device:TPU:1, one launch (start us, length us, event | category | flops | bytes accessed | tf_op | source)
XLA Modules:
  0.0 184.0 jit_solution(17896232364663788025)
XLA Ops:
  7.2 0.0 all-gather.2.cloned.1.call-start
  7.2 1.1 convert_element_type.20
  8.4 0.9 fusion.8.x_ref
  9.3 21.5 %shard_map.50 = f32[256,512]{1,0:T(8,128)} custom-call(f32[256,512]{1,0:T(8,128)} %fusion.8.x_ref), custom_call_target="tpu_custom_call" | custom-call | tf_op jit(solution)/shard_map/pallas_call | solution.py:91
  30.8 1.3 convert_multiply_fusion
  32.1 2.0 %fusion.2 = bf16[1,256,1024]{2,1,0:T(8,128)(2,1)} fusion(f32[256,512]{1,0:T(8,128)S(1)} %convert_multiply_fusion, bf16[1,256,1024]{2,1,0:T(8,128)(2,1)} %param.3), kind=kLoop, calls=%fused_computation.7 | loop fusion | flops 1048576 | bytes 1572864 | tf_op jit(solution)/shard_map/convert_element_type | solution.py:168
  34.1 0.0 all-gather.2.cloned.1.call-update
  34.1 0.7 pad_clamp_fusion
  34.8 0.1 fusion.17
  34.9 1.1 fusion.22
  36.0 102.1 %all-gather.2.cloned.1.call-done = bf16[1,8192,1024]{2,1,0:T(8,128)(2,1)} async-done(((bf16[1,256,1024]{2,1,0:T(8,128)(2,1)}), bf16[1,8192,1024]{2,1,0:T(8,128)(2,1)}) %all-gather.2.cloned.1.call-update) | async-done | bytes 16777232 | tf_op jit(solution)/shard_map/all_gather | solution.py:172
  138.1 8.5 %gather_fusion = bf16[16,1024]{1,0:T(8,128)(2,1)S(1)} fusion(bf16[8192,1024]{1,0:T(8,128)(2,1)} %bitcast.34, s32[1024]{0:T(1024)S(1)} %pad_clamp_fusion), kind=kCustom, calls=%fused_computation | custom fusion | bytes 65600 | tf_op jit(solution)/shard_map/jit(_take)/gather | solution.py:181
  146.6 1.9 %convolution_multiply_fusion = f32[32,256]{1,0:T(8,128)} fusion(bf16[1,256,1024]{2,1,0:T(8,128)(2,1)} %fusion.2, bf16[1,16,512]{2,1,0:T(8,128)(2,1)S(1)} %get-tuple-element.5, bf16[1,16,512]{2,1,0:T(8,128)(2,1)S(1)} %get-tuple-element.4, bf16[1,16,1024]{2,1,0:T(8,128)(2,1)S(1)} %bitcast.32), kind=kOutput, calls=%fused_computation.4 | convolution fusion | flops 16982016 | bytes 622592 | tf_op jit(solution)/shard_map/bkw,bjw->bkj/dot_general | solution.py:187
  148.6 11.6 %shard_map.51 = f32[8,2,16,256]{3,2,1,0:T(8,128)} custom-call(f32[2,16,256]{2,1,0:T(8,128)} %bitcast.33), custom_call_target="tpu_custom_call" | custom-call | tf_op jit(solution)/shard_map/pallas_call | solution.py:144
  160.2 2.4 %fusion = f32[16,256,32]{1,2,0:T(8,128)} fusion(f32[8,2,16,256]{3,2,1,0:T(8,128)} %shard_map.51, f32[8,1,32]{2,0,1:T(8,128)S(1)} %get-tuple-element.7, f32[8,1,32]{2,0,1:T(8,128)S(1)} %get-tuple-element.6), kind=kOutput, calls=%fused_computation.3 | convolution fusion | flops 25297408 | bytes 788480 | tf_op jit(solution)/shard_map/frsc,frl->scl/dot_general | solution.py:199
  162.6 14.5 %multiply_convert_fusion = bf16[512,8192]{1,0:T(8,128)(2,1)} fusion(bf16[1,256,512]{2,1,0:T(8,128)(2,1)S(1)} %get-tuple-element.3, bf16[1,256,512]{2,1,0:T(8,128)(2,1)S(1)} %get-tuple-element.2, bf16[1,256,1024]{2,1,0:T(8,128)(2,1)} %fusion.2, bf16[1,8192,1024]{2,1,0:T(8,128)(2,1)} %all-gather.2.cloned.1.call-done), kind=kOutput, calls=%fused_computation.1 | convolution fusion | flops 8601468928 | bytes 26214400 | tf_op jit(solution)/shard_map/bkw,bjw->bkj/dot_general | solution.py:173
  (3 shorter events, 0.0 us)
Async XLA Ops:
  7.2 130.9 %all-gather.2.cloned.1.call-start = ((), (), s32[]{:S(2)}) async-start(), calls=%async_computation | async-start | bytes 17301504 | tf_op jit(solution)/shard_map/all_gather | solution.py:172
Sparse Core Ops, SparseCore 0:
  34.2 103.8 all-gather.1

commit v3 on v2

--- a/solution.py
+++ b/solution.py
@@ -151,6 +151,69 @@
             pltpu.SemaphoreType.DMA((peers,)),
         ],
         compiler_params=pltpu.CompilerParams(collective_id=1, has_side_effects=True),
+    )(x)
+
+
+def _rows_kernel(chips, x_ref, out_ref, pair, held, send_sem, recv_sem):
+    me = lax.axis_index("grp")
+    band = lax.axis_index("freq")
+    core = me % 2
+    chip = me // 2
+    partner = me + 1 - 2 * core
+
+    def dev(g):
+        return (g, band)
+
+    barrier = pltpu.get_barrier_semaphore()
+    pl.semaphore_signal(barrier, inc=1, device_id=dev(partner), device_id_type=MESH)
+    for k in range(1, chips):
+        pl.semaphore_signal(barrier, inc=1, device_id=dev(((chip + k) % chips) * 2 + core), device_id_type=MESH)
+    pl.semaphore_wait(barrier, chips)
+
+    first = pltpu.make_async_remote_copy(
+        src_ref=x_ref, dst_ref=pair, send_sem=send_sem.at[0], recv_sem=recv_sem.at[0],
+        device_id=dev(partner), device_id_type=MESH,
+    )
+    first.start()
+    first.wait_recv()
+    first.wait_send()
+    held[chip] = (x_ref[...].astype(jnp.float32) + pair[...].astype(jnp.float32)).astype(held.dtype)
+    sent = []
+    for k in range(1, chips):
+        peer = (chip + k) % chips
+        copy = pltpu.make_async_remote_copy(
+            src_ref=held.at[chip], dst_ref=held.at[chip], send_sem=send_sem.at[1 + peer],
+            recv_sem=recv_sem.at[1 + chip], device_id=dev(peer * 2 + core), device_id_type=MESH,
+        )
+        copy.start()
+        sent.append(copy)
+    for k in range(1, chips):
+        src = (chip + chips - k) % chips
+        pltpu.make_async_remote_copy(
+            src_ref=held.at[src], dst_ref=held.at[src], send_sem=send_sem.at[1 + src],
+            recv_sem=recv_sem.at[1 + src], device_id=dev(src * 2 + core), device_id_type=MESH,
+        ).wait_recv()
+    for copy in sent:
+        copy.wait_send()
+    total = held[0].astype(jnp.float32)
+    for c in range(1, chips):
+        total = total + held[c].astype(jnp.float32)
+    out_ref[...] = total.astype(out_ref.dtype)
+
+
+def grp_rows_sum(x, chips):
+    return pl.pallas_call(
+        functools.partial(_rows_kernel, chips),
+        out_shape=jax.ShapeDtypeStruct(x.shape, x.dtype),
+        in_specs=[pl.BlockSpec(memory_space=pltpu.VMEM)],
+        out_specs=pl.BlockSpec(memory_space=pltpu.VMEM),
+        scratch_shapes=[
+            pltpu.VMEM(x.shape, x.dtype),
+            pltpu.VMEM((chips, *x.shape), x.dtype),
+            pltpu.SemaphoreType.DMA((chips + 1,)),
+            pltpu.SemaphoreType.DMA((chips + 1,)),
+        ],
+        compiler_params=pltpu.CompilerParams(collective_id=2, has_side_effects=True),
     )(x)
 
 
@@ -178,7 +241,13 @@
     )
 
     station_count = station_index.shape[0]
-    station_rows = jnp.take(peer_rows, station_index, axis=1, mode="clip")
+    group_index = lax.axis_index("grp")
+    local_rel = station_index - group_index * chan_count
+    selector = (local_rel[:, None] == jnp.arange(chan_count, dtype=jnp.int32)[None, :]).astype(
+        jnp.bfloat16
+    )
+    picked = jnp.einsum("sc,cw->sw", selector, whitened[0], preferred_element_type=jnp.float32)
+    station_rows = grp_rows_sum(picked.astype(jnp.bfloat16), lax.axis_size("grp") // 2)[None]
     station_swapped = jnp.concatenate(
         [station_rows[..., window_count:], -station_rows[..., :window_count]], axis=2
     )

time: 184 us -> 171 us (0.929)
  waiting for transfers between devices: 102 us -> 66.8 us
  Pallas kernels: 33.1 us -> 60.9 us
  local copies, waits for them, and re-layouts: 8.53 us -> 0 us
  matrix products: 18.9 us -> 20.8 us
    all_gather x1, waiting for transfers between devices: 102 us -> 66.7 us  [on_device(): peer_rows = lax.all_gather(whitened, 'grp', axis=1, tiled=True)]
    pallas_call x0 -> x1, Pallas kernels: none -> 29.6 us  [grp_rows_sum(): pl.pallas_call(functools.partial(_rows_kernel, chips), out_shape=jax.Shap...]
    gather x1 -> x0, local copies, waits for them, and re-layouts: 8.53 us -> none  [on_device(): station_rows = jnp.take(peer_rows, station_index, axis=1, mode='clip')]
    dot_general x0 -> x1, matrix products: none -> 1.88 us  [on_device(): jnp.einsum('sc,cw->sw', selector, whitened[0], preferred_element_type=jnp...]
  transfers between devices with their start and end apart: 1 -> 1, of which waited for: 1 -> 1; matrix products, arithmetic and copies ran while one was open for 1% -> 5% of each run, Pallas kernels for 0% -> 23%
where the time goes in v3:
time: 171 us
  waiting for transfers between devices  66.8 us (39%)
  Pallas kernels  60.9 us (36%)
  matrix products  20.8 us (12%)
  between operations  14.1 us (8%)
  other arithmetic  7.95 us (5%)
    all_gather x1, waiting for transfers between devices, on_device(): peer_rows = lax.all_gather(whitened, 'grp', axis=1, tiled=True)  66.7 us
    pallas_call x1, Pallas kernels, grp_rows_sum(): pl.pallas_call(functools.partial(_rows_kernel, chips), out_shape=jax.Shap...  29.6 us
    pallas_call x1, Pallas kernels, freq_psum(): pl.pallas_call(functools.partial(_psum_kernel, peers), out_shape=jax.Shap...  21.5 us
    dot_general x1, matrix products, on_device(): jnp.einsum('bkw,bjw->bkj', stacked, peer_rows, preferred_element_type=jnp...  14.5 us
    pallas_call x1, Pallas kernels, freq_gather(): pl.pallas_call(functools.partial(_gather_kernel, peers), out_shape=jax.Sh...  9.86 us
  transfers between devices with their start and end apart: 1, of which 1 were waited for; matrix products, arithmetic and copies ran while one was open for 5% of the time, Pallas kernels for 23%

profile of v3, /device:TPU:1, one launch (start us, length us, event | category | flops | bytes accessed | tf_op | source)
XLA Modules:
  0.0 170.6 jit_solution(3458375475856132688)
XLA Ops:
  7.2 0.0 all-gather.2.cloned.1.call-start
  7.2 1.1 convert_element_type.24
  8.4 0.9 fusion.12.x_ref
  9.3 21.5 %shard_map.50 = f32[256,512]{1,0:T(8,128)} custom-call(f32[256,512]{1,0:T(8,128)} %fusion.12.x_ref), custom_call_target="tpu_custom_call" | custom-call | tf_op jit(solution)/shard_map/pallas_call | solution.py:91
  30.8 1.3 convert_multiply_fusion
  32.1 2.0 %fusion.6 = bf16[1,256,1024]{2,1,0:T(8,128)(2,1)} fusion(f32[256,512]{1,0:T(8,128)S(1)} %convert_multiply_fusion, bf16[1,256,1024]{2,1,0:T(8,128)(2,1)} %param.3), kind=kLoop, calls=%fused_computation.9 | loop fusion | flops 1048576 | bytes 1572864 | tf_op jit(solution)/shard_map/convert_element_type | solution.py:231
  34.1 0.0 all-gather.2.cloned.1.call-update
  34.1 0.7 broadcast_subtract_fusion
  34.8 1.9 %convolution_convert_fusion.x_ref = bf16[16,1024]{1,0:T(8,128)(2,1)} fusion(bf16[1,256,1024]{2,1,0:T(8,128)(2,1)} %fusion.6, s32[16]{0:T(128)S(1)} %broadcast_subtract_fusion), kind=kOutput, calls=%fused_computation.5 | convolution fusion | flops 8409088 | bytes 557120 | tf_op jit(solution)/shard_map/sc,cw->sw/dot_general | solution.py:249
  36.6 29.6 %shard_map.51 = bf16[16,1024]{1,0:T(8,128)(2,1)} custom-call(bf16[16,1024]{1,0:T(8,128)(2,1)} %convolution_convert_fusion.x_ref), custom_call_target="tpu_custom_call" | custom-call | tf_op jit(solution)/shard_map/pallas_call | solution.py:205
  66.2 0.7 fusion.28
  67.0 1.9 %convolution_multiply_fusion = f32[32,256]{1,0:T(8,128)} fusion(bf16[1,256,1024]{2,1,0:T(8,128)(2,1)} %fusion.6, bf16[1,16,512]{2,1,0:T(8,128)(2,1)S(1)} %get-tuple-element.5, bf16[1,16,512]{2,1,0:T(8,128)(2,1)S(1)} %get-tuple-element.4, bf16[1,16,1024]{2,1,0:T(8,128)(2,1)} %bitcast.36), kind=kOutput, calls=%fused_computation.6 | convolution fusion | flops 16982016 | bytes 622592 | tf_op jit(solution)/shard_map/bkw,bjw->bkj/dot_general | solution.py:256
  68.9 9.9 %shard_map.52 = f32[8,2,16,256]{3,2,1,0:T(8,128)} custom-call(f32[2,16,256]{2,1,0:T(8,128)} %bitcast.37), custom_call_target="tpu_custom_call" | custom-call | tf_op jit(solution)/shard_map/pallas_call | solution.py:144
  78.8 0.1 fusion.23
  78.9 1.1 fusion.27
  80.0 2.4 %fusion.4 = f32[16,256,32]{1,2,0:T(8,128)} fusion(f32[8,2,16,256]{3,2,1,0:T(8,128)} %shard_map.52, f32[8,1,32]{2,0,1:T(8,128)S(1)} %get-tuple-element.7, f32[8,1,32]{2,0,1:T(8,128)S(1)} %get-tuple-element.6), kind=kOutput, calls=%fused_computation.4 | convolution fusion | flops 25297408 | bytes 788480 | tf_op jit(solution)/shard_map/frsc,frl->scl/dot_general | solution.py:268
  82.4 66.7 %all-gather.2.cloned.1.call-done = bf16[1,8192,1024]{2,1,0:T(8,128)(2,1)} async-done(((bf16[1,256,1024]{2,1,0:T(8,128)(2,1)}), bf16[1,8192,1024]{2,1,0:T(8,128)(2,1)}) %all-gather.2.cloned.1.call-update) | async-done | bytes 16777232 | tf_op jit(solution)/shard_map/all_gather | solution.py:235
  149.2 14.5 %multiply_convert_fusion = bf16[512,8192]{1,0:T(8,128)(2,1)} fusion(bf16[1,8192,1024]{2,1,0:T(8,128)(2,1)} %all-gather.2.cloned.1.call-done, bf16[1,256,512]{2,1,0:T(8,128)(2,1)S(1)} %get-tuple-element.3, bf16[1,256,512]{2,1,0:T(8,128)(2,1)S(1)} %get-tuple-element.2, bf16[1,256,1024]{2,1,0:T(8,128)(2,1)} %fusion.6), kind=kOutput, calls=%fused_computation.2 | convolution fusion | flops 8601468928 | bytes 26214400 | tf_op jit(solution)/shard_map/bkw,bjw->bkj/dot_general | solution.py:236
  (2 shorter events, 0.0 us)
Async XLA Ops:
  7.2 142.0 %all-gather.2.cloned.1.call-start = ((), (), s32[]{:S(2)}) async-start(), calls=%async_computation | async-start | bytes 17301504 | tf_op jit(solution)/shard_map/all_gather | solution.py:235
Sparse Core Ops, SparseCore 0:
  34.2 114.9 all-gather.1

commit v4 on v3

--- a/solution.py
+++ b/solution.py
@@ -214,6 +214,105 @@
             pltpu.SemaphoreType.DMA((chips + 1,)),
         ],
         compiler_params=pltpu.CompilerParams(collective_id=2, has_side_effects=True),
+    )(x)
+
+
+def _gather_grp_kernel(zs, x_ref, out_ref, send_sem, recv_ring, recv_x, recv_sib, local_sem):
+    me = lax.axis_index("grp")
+    band = lax.axis_index("freq")
+    c = me % 2
+    xl = (me // 2) % 2
+    z = me // 4
+    step = 1 - 2 * c
+    half = x_ref.shape[0] // 2
+
+    def blk(zz, xx, cc):
+        return (zz * 2 + xx) * 2 + cc
+
+    def dev(g):
+        return (g, band)
+
+    sib = blk(z, xl, 1 - c)
+    partner = blk(z, 1 - xl, c)
+    nxt = blk((z + step + zs) % zs, xl, c)
+    prv = blk((z - step + zs) % zs, xl, c)
+
+    barrier = pltpu.get_barrier_semaphore()
+    for g in (sib, partner, nxt, prv):
+        pl.semaphore_signal(barrier, inc=1, device_id=dev(g), device_id_type=MESH)
+    pl.semaphore_wait(barrier, 4)
+
+    sends = []
+
+    def send(src, dst, recv, g):
+        copy = pltpu.make_async_remote_copy(
+            src_ref=src, dst_ref=dst, send_sem=send_sem.at[len(sends)], recv_sem=recv,
+            device_id=dev(g), device_id_type=MESH,
+        )
+        copy.start()
+        sends.append(copy)
+
+    def wait(dst, recv, g):
+        pltpu.make_async_remote_copy(
+            src_ref=dst, dst_ref=dst, send_sem=send_sem.at[0], recv_sem=recv,
+            device_id=dev(g), device_id_type=MESH,
+        ).wait_recv()
+
+    def rows(b, h):
+        return out_ref.at[b, pl.ds(pl.multiple_of(h * half, half), half)]
+
+    own = blk(z, xl, c)
+    local = pltpu.make_async_copy(x_ref, out_ref.at[own], local_sem.at[0])
+    local.start()
+    send(x_ref, out_ref.at[own], recv_sib.at[0], sib)
+    send(x_ref, out_ref.at[own], recv_x.at[0], partner)
+    send(x_ref, out_ref.at[own], recv_ring.at[0, 0], nxt)
+    across = blk(z, 1 - xl, c)
+    wait(out_ref.at[across], recv_x.at[0], partner)
+    send(out_ref.at[across], out_ref.at[across], recv_sib.at[1], sib)
+    send(rows(across, xl), rows(across, xl), recv_ring.at[0, 1], nxt)
+    for s in range(zs - 1):
+        zo = (z - step * (s + 1) + 2 * zs) % zs
+        full = blk(zo, xl, c)
+        part = blk(zo, 1 - xl, c)
+        wait(out_ref.at[full], recv_ring.at[s, 0], prv)
+        wait(rows(part, xl), recv_ring.at[s, 1], prv)
+        if s < zs - 2:
+            send(out_ref.at[full], out_ref.at[full], recv_ring.at[s + 1, 0], nxt)
+            send(rows(part, xl), rows(part, xl), recv_ring.at[s + 1, 1], nxt)
+        send(rows(full, xl), rows(full, xl), recv_x.at[1 + s], partner)
+        send(out_ref.at[full], out_ref.at[full], recv_sib.at[2 + 2 * s], sib)
+        send(rows(part, xl), rows(part, xl), recv_sib.at[3 + 2 * s], sib)
+        wait(rows(part, 1 - xl), recv_x.at[1 + s], partner)
+        send(rows(part, 1 - xl), rows(part, 1 - xl), recv_sib.at[2 * zs + s], sib)
+    wait(out_ref.at[sib], recv_sib.at[0], sib)
+    wait(out_ref.at[blk(z, 1 - xl, 1 - c)], recv_sib.at[1], sib)
+    for s in range(zs - 1):
+        zo = (z + step * (s + 1) + 2 * zs) % zs
+        wait(out_ref.at[blk(zo, xl, 1 - c)], recv_sib.at[2 + 2 * s], sib)
+        wait(rows(blk(zo, 1 - xl, 1 - c), xl), recv_sib.at[3 + 2 * s], sib)
+        wait(rows(blk(zo, 1 - xl, 1 - c), 1 - xl), recv_sib.at[2 * zs + s], sib)
+    local.wait()
+    for copy in sends:
+        copy.wait_send()
+
+
+def grp_gather(x, zs):
+    groups = lax.axis_size("grp")
+    rows, cols = x.shape
+    return pl.pallas_call(
+        functools.partial(_gather_grp_kernel, zs),
+        out_shape=jax.ShapeDtypeStruct((groups, rows, cols), x.dtype),
+        in_specs=[pl.BlockSpec(memory_space=pl.ANY)],
+        out_specs=pl.BlockSpec(memory_space=pl.ANY),
+        scratch_shapes=[
+            pltpu.SemaphoreType.DMA((6 * zs,)),
+            pltpu.SemaphoreType.DMA((zs - 1, 2)),
+            pltpu.SemaphoreType.DMA((zs,)),
+            pltpu.SemaphoreType.DMA((3 * zs - 1,)),
+            pltpu.SemaphoreType.DMA((1,)),
+        ],
+        compiler_params=pltpu.CompilerParams(collective_id=3, has_side_effects=True),
     )(x)
 
 
@@ -232,7 +331,9 @@
     swapped = jnp.concatenate([whitened[..., window_count:], -whitened[..., :window_count]], axis=2)
     stacked = jnp.concatenate([whitened, swapped], axis=1)
     scaling = 1.0 / math.sqrt(window_count)
-    peer_rows = lax.all_gather(whitened, "grp", axis=1, tiled=True)
+    peer_rows = grp_gather(whitened[0], lax.axis_size("grp") // 4).reshape(
+        bin_count, lax.axis_size("grp") * chan_count, double_width
+    )
     product = jnp.einsum("bkw,bjw->bkj", stacked, peer_rows, preferred_element_type=jnp.float32)
     cross = (
         (product * scaling)

time: 171 us -> 192 us (1.12)
  Pallas kernels: 60.9 us -> 153 us
  waiting for transfers between devices: 66.8 us -> 0 us
  between operations: 14.1 us -> 0.72 us
  matrix products: 20.8 us -> 30.7 us
    pallas_call x0 -> x1, Pallas kernels: none -> 100 us  [grp_gather(): pl.pallas_call(functools.partial(_gather_grp_kernel, zs), out_shape=jax.S...]
    all_gather x1 -> x0, waiting for transfers between devices: 66.7 us -> none  [on_device(): peer_rows = lax.all_gather(whitened, 'grp', axis=1, tiled=True)]
    dot_general x1, matrix products: 14.5 us -> 25.8 us  [on_device(): jnp.einsum('bkw,bjw->bkj', stacked, peer_rows, preferred_element_type=jnp...]
    pallas_call x1, Pallas kernels: 29.6 us -> 21.9 us  [grp_rows_sum(): pl.pallas_call(functools.partial(_rows_kernel, chips), out_shape=jax.Shap...]
  transfers between devices with their start and end apart: 1 -> 0, of which waited for: 1 -> 0; matrix products, arithmetic and copies ran while one was open for 5% -> 0% of each run, Pallas kernels for 23% -> 0%
where the time goes in v4:
time: 192 us; the launch traced here: 191 us
  Pallas kernels  153 us (80%)
  matrix products  30.7 us (16%)
  other arithmetic  6.23 us (3%)
    pallas_call x1, Pallas kernels, grp_gather(): pl.pallas_call(functools.partial(_gather_grp_kernel, zs), out_shape=jax.S...  100 us
    dot_general x1, matrix products, on_device(): jnp.einsum('bkw,bjw->bkj', stacked, peer_rows, preferred_element_type=jnp...  25.8 us
    pallas_call x1, Pallas kernels, grp_rows_sum(): pl.pallas_call(functools.partial(_rows_kernel, chips), out_shape=jax.Shap...  21.9 us
    pallas_call x1, Pallas kernels, freq_psum(): pl.pallas_call(functools.partial(_psum_kernel, peers), out_shape=jax.Shap...  21.5 us
    pallas_call x1, Pallas kernels, freq_gather(): pl.pallas_call(functools.partial(_gather_kernel, peers), out_shape=jax.Sh...  9.36 us

profile of v4, /device:TPU:1, one launch (start us, length us, event | category | flops | bytes accessed | tf_op | source)
XLA Modules:
  0.0 190.9 jit_solution(1109670486846438283)
XLA Ops:
  0.6 1.1 convert_element_type.24
  1.8 0.9 fusion.8.x_ref
  2.7 21.5 %shard_map.50 = f32[256,512]{1,0:T(8,128)} custom-call(f32[256,512]{1,0:T(8,128)} %fusion.8.x_ref), custom_call_target="tpu_custom_call" | custom-call | tf_op jit(solution)/shard_map/pallas_call | solution.py:91
  24.2 1.3 convert_multiply_fusion
  25.5 2.0 %fusion.2 = bf16[1,256,1024]{2,1,0:T(8,128)(2,1)} fusion(f32[256,512]{1,0:T(8,128)S(1)} %convert_multiply_fusion, bf16[1,256,1024]{2,1,0:T(8,128)(2,1)} %param.3), kind=kLoop, calls=%fused_computation.7 | loop fusion | flops 1048576 | bytes 1572864 | tf_op jit(solution)/shard_map/convert_element_type | solution.py:330
  27.5 0.0 copy-start
  27.5 100.5 %shard_map.51 = bf16[32,256,1024]{2,1,0:T(8,128)(2,1)} custom-call(bf16[256,1024]{1,0:T(8,128)(2,1)} %bitcast.33), custom_call_target="tpu_custom_call" | custom-call | tf_op jit(solution)/shard_map/pallas_call | solution.py:303
  128.0 0.0 copy-done
  128.0 0.0 copy-start.1
  128.0 25.8 %multiply_convert_fusion = bf16[512,8192]{1,0:T(8,128)(2,1)} fusion(bf16[8192,1024]{1,0:T(8,128)(2,1)} %bitcast.32, bf16[1,256,512]{2,1,0:T(8,128)(2,1)S(1)} %get-tuple-element.3, bf16[1,256,512]{2,1,0:T(8,128)(2,1)S(1)} %get-tuple-element.2, bf16[1,256,1024]{2,1,0:T(8,128)(2,1)S(1)} %copy-done), kind=kOutput, calls=%fused_computation | convolution fusion | flops 8601468928 | bytes 26214400 | tf_op jit(solution)/shard_map/bkw,bjw->bkj/dot_general | solution.py:337
  153.8 0.0 copy-done.1
  153.8 0.8 convolution_convert_fusion.x_ref
  154.6 21.9 %shard_map.52 = bf16[16,1024]{1,0:T(8,128)(2,1)} custom-call(bf16[16,1024]{1,0:T(8,128)(2,1)} %convolution_convert_fusion.x_ref), custom_call_target="tpu_custom_call" | custom-call | tf_op jit(solution)/shard_map/pallas_call | solution.py:205
  176.5 0.7 fusion.24
  177.3 1.6 convolution_multiply_fusion
  178.9 9.4 %shard_map.53 = f32[8,2,16,256]{3,2,1,0:T(8,128)} custom-call(f32[2,16,256]{2,1,0:T(8,128)} %bitcast.36), custom_call_target="tpu_custom_call" | custom-call | tf_op jit(solution)/shard_map/pallas_call | solution.py:144
  188.3 0.1 fusion.17
  188.4 2.4 %fusion = f32[16,256,32]{1,2,0:T(8,128)} fusion(f32[8,2,16,256]{3,2,1,0:T(8,128)} %shard_map.53, f32[8,1,32]{2,0,1:T(8,128)S(1)} %get-tuple-element.7, f32[8,1,32]{2,0,1:T(8,128)S(1)} %get-tuple-element.6), kind=kOutput, calls=%fused_computation.2 | convolution fusion | flops 25297408 | bytes 788480 | tf_op jit(solution)/shard_map/frsc,frl->scl/dot_general | solution.py:369
  (4 shorter events, 0.1 us)
Async XLA Ops:
  27.5 100.5 %copy-start = (bf16[1,256,1024]{2,1,0:T(8,128)(2,1)S(1)}, bf16[1,256,1024]{2,1,0:T(8,128)(2,1)}, u32[]{:S(2)}) copy-start(bf16[1,256,1024]{2,1,0:T(8,128)(2,1)} %fusion.2) | copy-start | bytes 1572868
  128.0 25.8 %copy-start.1 = (s32[16]{0:T(128)S(1)}, s32[16]{0:T(128)}, u32[]{:S(2)}) copy-start(s32[16]{0:T(128)} %param.5) | copy-start | bytes 196

commit v5 on v4

--- a/solution.py
+++ b/solution.py
@@ -217,14 +217,16 @@
     )(x)
 
 
-def _gather_grp_kernel(zs, x_ref, out_ref, send_sem, recv_ring, recv_x, recv_sib, local_sem):
+def _cross_kernel(zs, scaling, x_ref, left_ref, sel_ref, cross_ref, rows_ref, held, stage, picked,
+                  send_sem, recv_ring, recv_x, recv_sib, out_sem):
     me = lax.axis_index("grp")
     band = lax.axis_index("freq")
     c = me % 2
     xl = (me // 2) % 2
     z = me // 4
     step = 1 - 2 * c
-    half = x_ref.shape[0] // 2
+    width = x_ref.shape[0]
+    half = width // 2
 
     def blk(zz, xx, cc):
         return (zz * 2 + xx) * 2 + cc
@@ -243,6 +245,7 @@
     pl.semaphore_wait(barrier, 4)
 
     sends = []
+    outs = []
 
     def send(src, dst, recv, g):
         copy = pltpu.make_async_remote_copy(
@@ -259,61 +262,100 @@
         ).wait_recv()
 
     def rows(b, h):
-        return out_ref.at[b, pl.ds(pl.multiple_of(h * half, half), half)]
-
+        return held.at[b, pl.ds(pl.multiple_of(h * half, half), half)]
+
+    def compute(b):
+        block = held[b]
+        prod = lax.dot_general(
+            left_ref[...], block, (((1,), (1,)), ((), ())), preferred_element_type=jnp.float32
+        )
+        slot = len(outs) % 2
+        if len(outs) >= 2:
+            outs[-2].wait()
+        stage[slot] = (prod * scaling).astype(stage.dtype).reshape(stage.shape[1:])
+        copy = pltpu.make_async_copy(
+            stage.at[slot], cross_ref.at[:, :, pl.ds(pl.multiple_of(b * width, width), width)], out_sem.at[slot]
+        )
+        copy.start()
+        outs.append(copy)
+        picked[...] += jnp.dot(
+            sel_ref[:, pl.ds(pl.multiple_of(b * width, width), width)], block,
+            preferred_element_type=jnp.float32,
+        )
+
+    picked[...] = jnp.zeros_like(picked)
     own = blk(z, xl, c)
-    local = pltpu.make_async_copy(x_ref, out_ref.at[own], local_sem.at[0])
-    local.start()
-    send(x_ref, out_ref.at[own], recv_sib.at[0], sib)
-    send(x_ref, out_ref.at[own], recv_x.at[0], partner)
-    send(x_ref, out_ref.at[own], recv_ring.at[0, 0], nxt)
+    held[own] = x_ref[...]
+    send(x_ref, held.at[own], recv_x.at[0], partner)
+    send(x_ref, held.at[own], recv_sib.at[0], sib)
+    send(x_ref.at[pl.ds(0, half)], rows(own, 0), recv_ring.at[0, 0], nxt)
+    send(x_ref.at[pl.ds(half, half)], rows(own, 1), recv_ring.at[0, 1], nxt)
+    compute(own)
     across = blk(z, 1 - xl, c)
-    wait(out_ref.at[across], recv_x.at[0], partner)
-    send(out_ref.at[across], out_ref.at[across], recv_sib.at[1], sib)
-    send(rows(across, xl), rows(across, xl), recv_ring.at[0, 1], nxt)
+    wait(held.at[across], recv_x.at[0], partner)
+    send(rows(across, xl), rows(across, xl), recv_ring.at[0, 2], nxt)
+    send(held.at[across], held.at[across], recv_sib.at[1], sib)
+    compute(across)
+    wait(held.at[sib], recv_sib.at[0], sib)
+    compute(sib)
+    sib_across = blk(z, 1 - xl, 1 - c)
+    wait(held.at[sib_across], recv_sib.at[1], sib)
+    compute(sib_across)
     for s in range(zs - 1):
         zo = (z - step * (s + 1) + 2 * zs) % zs
         full = blk(zo, xl, c)
         part = blk(zo, 1 - xl, c)
-        wait(out_ref.at[full], recv_ring.at[s, 0], prv)
-        wait(rows(part, xl), recv_ring.at[s, 1], prv)
-        if s < zs - 2:
-            send(out_ref.at[full], out_ref.at[full], recv_ring.at[s + 1, 0], nxt)
-            send(rows(part, xl), rows(part, xl), recv_ring.at[s + 1, 1], nxt)
+        pieces = ((full, 0), (full, 1), (part, xl))
+        for k, (b, h) in enumerate(pieces):
+            wait(rows(b, h), recv_ring.at[s, k], prv)
+            if s < zs - 2:
+                send(rows(b, h), rows(b, h), recv_ring.at[s + 1, k], nxt)
+            send(rows(b, h), rows(b, h), recv_sib.at[2 + 3 * s + k], sib)
         send(rows(full, xl), rows(full, xl), recv_x.at[1 + s], partner)
-        send(out_ref.at[full], out_ref.at[full], recv_sib.at[2 + 2 * s], sib)
-        send(rows(part, xl), rows(part, xl), recv_sib.at[3 + 2 * s], sib)
+        compute(full)
         wait(rows(part, 1 - xl), recv_x.at[1 + s], partner)
-        send(rows(part, 1 - xl), rows(part, 1 - xl), recv_sib.at[2 * zs + s], sib)
-    wait(out_ref.at[sib], recv_sib.at[0], sib)
-    wait(out_ref.at[blk(z, 1 - xl, 1 - c)], recv_sib.at[1], sib)
-    for s in range(zs - 1):
-        zo = (z + step * (s + 1) + 2 * zs) % zs
-        wait(out_ref.at[blk(zo, xl, 1 - c)], recv_sib.at[2 + 2 * s], sib)
-        wait(rows(blk(zo, 1 - xl, 1 - c), xl), recv_sib.at[3 + 2 * s], sib)
-        wait(rows(blk(zo, 1 - xl, 1 - c), 1 - xl), recv_sib.at[2 * zs + s], sib)
-    local.wait()
+        send(rows(part, 1 - xl), rows(part, 1 - xl), recv_sib.at[2 + 3 * (zs - 1) + s], sib)
+        compute(part)
+        zt = (z + step * (s + 1) + 2 * zs) % zs
+        sfull = blk(zt, xl, 1 - c)
+        spart = blk(zt, 1 - xl, 1 - c)
+        for k, (b, h) in enumerate(((sfull, 0), (sfull, 1), (spart, xl))):
+            wait(rows(b, h), recv_sib.at[2 + 3 * s + k], sib)
+        compute(sfull)
+        wait(rows(spart, 1 - xl), recv_sib.at[2 + 3 * (zs - 1) + s], sib)
+        compute(spart)
+    rows_ref[...] = picked[...].astype(rows_ref.dtype)
+    for copy in outs[-2:]:
+        copy.wait()
     for copy in sends:
         copy.wait_send()
 
 
-def grp_gather(x, zs):
+def grp_cross(whitened, left, selector, scaling, zs):
     groups = lax.axis_size("grp")
-    rows, cols = x.shape
+    width, cols = whitened.shape
     return pl.pallas_call(
-        functools.partial(_gather_grp_kernel, zs),
-        out_shape=jax.ShapeDtypeStruct((groups, rows, cols), x.dtype),
-        in_specs=[pl.BlockSpec(memory_space=pl.ANY)],
-        out_specs=pl.BlockSpec(memory_space=pl.ANY),
+        functools.partial(_cross_kernel, zs, scaling),
+        out_shape=(
+            jax.ShapeDtypeStruct((2, width, groups * width), whitened.dtype),
+            jax.ShapeDtypeStruct((selector.shape[0], cols), whitened.dtype),
+        ),
+        in_specs=[pl.BlockSpec(memory_space=pltpu.VMEM)] * 3,
+        out_specs=(pl.BlockSpec(memory_space=pl.ANY), pl.BlockSpec(memory_space=pltpu.VMEM)),
         scratch_shapes=[
-            pltpu.SemaphoreType.DMA((6 * zs,)),
-            pltpu.SemaphoreType.DMA((zs - 1, 2)),
+            pltpu.VMEM((groups, width, cols), whitened.dtype),
+            pltpu.VMEM((2, 2, width, width), whitened.dtype),
+            pltpu.VMEM((selector.shape[0], cols), jnp.float32),
+            pltpu.SemaphoreType.DMA((8 * zs + 8,)),
+            pltpu.SemaphoreType.DMA((zs - 1, 3)),
             pltpu.SemaphoreType.DMA((zs,)),
-            pltpu.SemaphoreType.DMA((3 * zs - 1,)),
-            pltpu.SemaphoreType.DMA((1,)),
+            pltpu.SemaphoreType.DMA((2 + 4 * (zs - 1),)),
+            pltpu.SemaphoreType.DMA((2,)),
         ],
-        compiler_params=pltpu.CompilerParams(collective_id=3, has_side_effects=True),
-    )(x)
+        compiler_params=pltpu.CompilerParams(
+            collective_id=3, has_side_effects=True, vmem_limit_bytes=56 * 1024 * 1024
+        ),
+    )(whitened, left, selector)
 
 
 def on_device(spectra, valid, station_index):
@@ -331,24 +373,16 @@
     swapped = jnp.concatenate([whitened[..., window_count:], -whitened[..., :window_count]], axis=2)
     stacked = jnp.concatenate([whitened, swapped], axis=1)
     scaling = 1.0 / math.sqrt(window_count)
-    peer_rows = grp_gather(whitened[0], lax.axis_size("grp") // 4).reshape(
-        bin_count, lax.axis_size("grp") * chan_count, double_width
-    )
-    product = jnp.einsum("bkw,bjw->bkj", stacked, peer_rows, preferred_element_type=jnp.float32)
-    cross = (
-        (product * scaling)
-        .astype(jnp.bfloat16)
-        .reshape(bin_count, 2, chan_count, peer_rows.shape[1])
-    )
-
     station_count = station_index.shape[0]
-    group_index = lax.axis_index("grp")
-    local_rel = station_index - group_index * chan_count
-    selector = (local_rel[:, None] == jnp.arange(chan_count, dtype=jnp.int32)[None, :]).astype(
+    total_chans = lax.axis_size("grp") * chan_count
+    selector = (station_index[:, None] == jnp.arange(total_chans, dtype=jnp.int32)[None, :]).astype(
         jnp.bfloat16
     )
-    picked = jnp.einsum("sc,cw->sw", selector, whitened[0], preferred_element_type=jnp.float32)
-    station_rows = grp_rows_sum(picked.astype(jnp.bfloat16), lax.axis_size("grp") // 2)[None]
+    cross, station_rows = grp_cross(
+        whitened[0], stacked[0], selector, scaling, lax.axis_size("grp") // 4
+    )
+    cross = cross[None]
+    station_rows = station_rows[None]
     station_swapped = jnp.concatenate(
         [station_rows[..., window_count:], -station_rows[..., :window_count]], axis=2
     )

time: 192 us -> 149 us (0.78)
  matrix products: 30.7 us -> 4.38 us
  Pallas kernels: 153 us -> 129 us
  local copies, waits for them, and re-layouts: 0.01 us -> 7.79 us
    dot_general x2 -> x0, matrix products: 26.6 us -> none  [the longest x1 25.8 us: on_device(): jnp.einsum('bkw,bjw->bkj', stacked, peer_rows, preferred_element_type=jnp...]
    pallas_call x2 -> x1, Pallas kernels: 122 us -> 98.4 us  [grp_cross(): pl.pallas_call(functools.partial(_cross_kernel, zs, scaling), out_shape=(...]
    unnamed x4 -> x9, local copies, waits for them, and re-layouts: 0.01 us -> 7.79 us
where the time goes in v5:
time: 149 us; the launch traced here: 148 us
  Pallas kernels  129 us (87%)
  local copies, waits for them, and re-layouts  7.79 us (5%)
  other arithmetic  6.21 us (4%)
  matrix products  4.38 us (3%)
    pallas_call x1, Pallas kernels, grp_cross(): pl.pallas_call(functools.partial(_cross_kernel, zs, scaling), out_shape=(...  98.4 us
    pallas_call x1, Pallas kernels, freq_psum(): pl.pallas_call(functools.partial(_psum_kernel, peers), out_shape=jax.Shap...  21.5 us
    pallas_call x1, Pallas kernels, freq_gather(): pl.pallas_call(functools.partial(_gather_kernel, peers), out_shape=jax.Sh...  9.38 us
    unnamed x9, local copies, waits for them, and re-layouts  7.79 us

profile of v5, /device:TPU:1, one launch (start us, length us, event | category | flops | bytes accessed | tf_op | source)
XLA Modules:
  0.0 148.4 jit_solution(7359289926116241646)
XLA Ops:
  0.6 0.0 copy-start.2
  0.6 1.2 convert_element_type.19
  1.8 0.0 copy-start.1
  1.9 0.9 fusion.4.x_ref
  2.8 21.5 %shard_map.50 = f32[256,512]{1,0:T(8,128)} custom-call(f32[256,512]{1,0:T(8,128)} %fusion.4.x_ref), custom_call_target="tpu_custom_call" | custom-call | tf_op jit(solution)/shard_map/pallas_call | solution.py:91
  24.3 0.0 copy-done.2
  24.3 1.2 convert_multiply_fusion
  25.4 0.0 copy-done.1
  25.4 0.0 copy-start.3
  25.5 0.1 fusion.2
  25.6 0.0 copy-start
  25.7 1.1 maximum_bitcast_fusion.1.left_ref
  26.8 0.0 copy-done.3
  26.8 0.8 fusion.5.sel_ref
  27.6 0.0 copy-done
  27.6 98.4 %shard_map.51 = (bf16[2,256,8192]{2,1,0:T(8,128)(2,1)}, bf16[16,1024]{1,0:T(8,128)(2,1)}) custom-call(bf16[256,1024]{1,0:T(8,128)(2,1)} %bitcast.27, bf16[512,1024]{1,0:T(8,128)(2,1)} %maximum_bitcast_fusion.1.left_ref, bf16[16,8192]{1,0:T(8,128)(2,1)} %fusion.5.sel_ref), custom_call_target="tpu_custom_call" | custom-call | tf_op jit(solution)/shard_map/pallas_call | solution.py:337
  126.0 0.7 fusion.18
  126.7 1.9 %convolution_multiply_fusion = f32[32,256]{1,0:T(8,128)} fusion(bf16[1,16,512]{2,1,0:T(8,128)(2,1)S(1)} %get-tuple-element.9, bf16[1,16,512]{2,1,0:T(8,128)(2,1)S(1)} %get-tuple-element.8, bf16[1,16,1024]{2,1,0:T(8,128)(2,1)} %bitcast.31, bf16[1,256,1024]{2,1,0:T(8,128)(2,1)} %copy-done), kind=kOutput, calls=%fused_computation.2 | convolution fusion | flops 16982016 | bytes 622592 | tf_op jit(solution)/shard_map/bkw,bjw->bkj/dot_general | solution.py:391
  128.7 9.4 %shard_map.52 = f32[8,2,16,256]{3,2,1,0:T(8,128)} custom-call(f32[2,16,256]{2,1,0:T(8,128)} %bitcast.29), custom_call_target="tpu_custom_call" | custom-call | tf_op jit(solution)/shard_map/pallas_call | solution.py:144
  138.1 0.1 fusion.13
  138.2 2.4 %fusion = f32[16,256,32]{1,2,0:T(8,128)} fusion(f32[8,2,16,256]{3,2,1,0:T(8,128)} %shard_map.52, f32[8,1,32]{2,0,1:T(8,128)S(1)} %get-tuple-element.11, f32[8,1,32]{2,0,1:T(8,128)S(1)} %get-tuple-element.10), kind=kOutput, calls=%fused_computation.1 | convolution fusion | flops 25297408 | bytes 788480 | tf_op jit(solution)/shard_map/frsc,frl->scl/dot_general | solution.py:403
  140.6 7.8 %copy.10 = bf16[1,2,256,8192]{3,2,1,0:T(8,128)(2,1)} copy(bf16[1,2,256,8192]{3,2,1,0:T(8,128)(2,1)} %bitcast.28) | data formatting | bytes 16777216
  (3 shorter events, 0.1 us)
Async XLA Ops:
  0.6 23.6 %copy-start.2 = (s32[256,512]{1,0:T(8,128)S(1)}, s32[256,512]{1,0:T(8,128)}, u32[]{:S(2)}) copy-start(s32[256,512]{1,0:T(8,128)} %param.4) | copy-start | bytes 1572868
  1.8 23.6 %copy-start.1 = (bf16[1,256,1024]{2,1,0:T(8,128)(2,1)S(1)}, bf16[1,256,1024]{2,1,0:T(8,128)(2,1)}, u32[]{:S(2)}) copy-start(bf16[1,256,1024]{2,1,0:T(8,128)(2,1)} %param.3) | copy-start | bytes 1572868
  25.4 1.3 copy-start.3
  25.6 2.0 %copy-start = (bf16[1,256,1024]{2,1,0:T(8,128)(2,1)}, bf16[1,256,1024]{2,1,0:T(8,128)(2,1)S(1)}, u32[]{:S(2)}) copy-start(bf16[1,256,1024]{2,1,0:T(8,128)(2,1)S(1)} %fusion.2) | copy-start | bytes 1572868

commit v6 on v5

--- a/solution.py
+++ b/solution.py
@@ -217,8 +217,8 @@
     )(x)
 
 
-def _cross_kernel(zs, scaling, x_ref, left_ref, sel_ref, cross_ref, rows_ref, held, stage, picked,
-                  send_sem, recv_ring, recv_x, recv_sib, out_sem):
+def _cross_kernel(zs, bands, scaling, x_ref, left_ref, sel_ref, cross_ref, bins_ref, held, stage, picked,
+                  send_sem, recv_ring, recv_x, recv_sib, out_sem, recv_f):
     me = lax.axis_index("grp")
     band = lax.axis_index("freq")
     c = me % 2
@@ -242,7 +242,9 @@
     barrier = pltpu.get_barrier_semaphore()
     for g in (sib, partner, nxt, prv):
         pl.semaphore_signal(barrier, inc=1, device_id=dev(g), device_id_type=MESH)
-    pl.semaphore_wait(barrier, 4)
+    for k in range(1, bands):
+        pl.semaphore_signal(barrier, inc=1, device_id=(me, (band + k) % bands), device_id_type=MESH)
+    pl.semaphore_wait(barrier, 4 + bands - 1)
 
     sends = []
     outs = []
@@ -324,7 +326,28 @@
         compute(sfull)
         wait(rows(spart, 1 - xl), recv_sib.at[2 + 3 * (zs - 1) + s], sib)
         compute(spart)
-    rows_ref[...] = picked[...].astype(rows_ref.dtype)
+    station = picked[...]
+    wide = station.shape[1] // 2
+    swapped = jnp.concatenate([station[:, wide:], -station[:, :wide]], axis=1)
+    left = jnp.concatenate([station, swapped], axis=0).astype(x_ref.dtype)
+    values = lax.dot_general(
+        left, x_ref[...], (((1,), (1,)), ((), ())), preferred_element_type=jnp.float32
+    ) * scaling
+    bins_ref[band] = values.reshape(bins_ref.shape[1:])
+    for k in range(1, bands):
+        peer = (band + k) % bands
+        copy = pltpu.make_async_remote_copy(
+            src_ref=bins_ref.at[band], dst_ref=bins_ref.at[band], send_sem=send_sem.at[len(sends)],
+            recv_sem=recv_f.at[band], device_id=(me, peer), device_id_type=MESH,
+        )
+        copy.start()
+        sends.append(copy)
+    for k in range(1, bands):
+        src = (band + bands - k) % bands
+        pltpu.make_async_remote_copy(
+            src_ref=bins_ref.at[src], dst_ref=bins_ref.at[src], send_sem=send_sem.at[0],
+            recv_sem=recv_f.at[src], device_id=(me, src), device_id_type=MESH,
+        ).wait_recv()
     for copy in outs[-2:]:
         copy.wait()
     for copy in sends:
@@ -333,12 +356,13 @@
 
 def grp_cross(whitened, left, selector, scaling, zs):
     groups = lax.axis_size("grp")
+    bands = lax.axis_size("freq")
     width, cols = whitened.shape
     return pl.pallas_call(
-        functools.partial(_cross_kernel, zs, scaling),
+        functools.partial(_cross_kernel, zs, bands, scaling),
         out_shape=(
             jax.ShapeDtypeStruct((2, width, groups * width), whitened.dtype),
-            jax.ShapeDtypeStruct((selector.shape[0], cols), whitened.dtype),
+            jax.ShapeDtypeStruct((bands, 2, selector.shape[0], width), jnp.float32),
         ),
         in_specs=[pl.BlockSpec(memory_space=pltpu.VMEM)] * 3,
         out_specs=(pl.BlockSpec(memory_space=pl.ANY), pl.BlockSpec(memory_space=pltpu.VMEM)),
@@ -346,11 +370,12 @@
             pltpu.VMEM((groups, width, cols), whitened.dtype),
             pltpu.VMEM((2, 2, width, width), whitened.dtype),
             pltpu.VMEM((selector.shape[0], cols), jnp.float32),
-            pltpu.SemaphoreType.DMA((8 * zs + 8,)),
+            pltpu.SemaphoreType.DMA((8 * zs + 16,)),
             pltpu.SemaphoreType.DMA((zs - 1, 3)),
             pltpu.SemaphoreType.DMA((zs,)),
             pltpu.SemaphoreType.DMA((2 + 4 * (zs - 1),)),
             pltpu.SemaphoreType.DMA((2,)),
+            pltpu.SemaphoreType.DMA((bands,)),
         ],
         compiler_params=pltpu.CompilerParams(
             collective_id=3, has_side_effects=True, vmem_limit_bytes=56 * 1024 * 1024
@@ -378,21 +403,10 @@
     selector = (station_index[:, None] == jnp.arange(total_chans, dtype=jnp.int32)[None, :]).astype(
         jnp.bfloat16
     )
-    cross, station_rows = grp_cross(
+    cross, all_bins = grp_cross(
         whitened[0], stacked[0], selector, scaling, lax.axis_size("grp") // 4
     )
     cross = cross[None]
-    station_rows = station_rows[None]
-    station_swapped = jnp.concatenate(
-        [station_rows[..., window_count:], -station_rows[..., :window_count]], axis=2
-    )
-    station_left = jnp.concatenate([station_rows, station_swapped], axis=1)
-    kernel = (
-        jnp.einsum("bkw,bjw->bkj", station_left, whitened, preferred_element_type=jnp.float32)
-        * scaling
-    )
-    kernel = kernel.reshape(2, station_count, chan_count)
-    all_bins = freq_gather(kernel, freq_count)
 
     lag_share = LAGS // freq_count
     freq_index = lax.axis_index("freq")

time: 149 us -> 143 us (0.960)
  Pallas kernels: 129 us -> 126 us
  matrix products: 4.38 us -> 2.44 us
    pallas_call x2 -> x1, Pallas kernels: 108 us -> 105 us  [grp_cross(): pl.pallas_call(functools.partial(_cross_kernel, zs, bands, scaling), out_...]
    dot_general x1 -> x0, matrix products: 1.94 us -> none  [on_device(): jnp.einsum('bkw,bjw->bkj', station_left, whitened, preferred_element_type...]
where the time goes in v6:
time: 143 us
  Pallas kernels  126 us (88%)
  local copies, waits for them, and re-layouts  7.79 us (5%)
  other arithmetic  5.47 us (4%)
  matrix products  2.44 us (2%)
    pallas_call x1, Pallas kernels, grp_cross(): pl.pallas_call(functools.partial(_cross_kernel, zs, bands, scaling), out_...  105 us
    pallas_call x1, Pallas kernels, freq_psum(): pl.pallas_call(functools.partial(_psum_kernel, peers), out_shape=jax.Shap...  21.5 us
    unnamed x9, local copies, waits for them, and re-layouts  7.79 us

profile of v6, /device:TPU:1, one launch (start us, length us, event | category | flops | bytes accessed | tf_op | source)
XLA Modules:
  0.0 142.9 jit_solution(14502625322566919288)
XLA Ops:
  0.6 0.0 copy-start.2
  0.6 1.2 convert_element_type.19
  1.8 0.0 copy-start.1
  1.9 0.9 fusion.4.x_ref
  2.8 21.5 %shard_map.50 = f32[256,512]{1,0:T(8,128)} custom-call(f32[256,512]{1,0:T(8,128)} %fusion.4.x_ref), custom_call_target="tpu_custom_call" | custom-call | tf_op jit(solution)/shard_map/pallas_call | solution.py:91
  24.3 0.0 copy-done.2
  24.3 1.2 convert_multiply_fusion
  25.4 0.0 copy-done.1
  25.4 0.0 copy-start.3
  25.5 0.1 fusion.2
  25.6 0.0 copy-start
  25.7 1.1 maximum_bitcast_fusion.1.left_ref
  26.8 0.0 copy-done.3
  26.8 0.8 fusion.5.sel_ref
  27.6 0.0 copy-done
  27.6 104.9 %shard_map.51 = (bf16[2,256,8192]{2,1,0:T(8,128)(2,1)}, f32[8,2,16,256]{3,2,1,0:T(8,128)}) custom-call(bf16[256,1024]{1,0:T(8,128)(2,1)} %bitcast.20, bf16[512,1024]{1,0:T(8,128)(2,1)} %maximum_bitcast_fusion.1.left_ref, bf16[16,8192]{1,0:T(8,128)(2,1)} %fusion.5.sel_ref), custom_call_target="tpu_custom_call" | custom-call | tf_op jit(solution)/shard_map/pallas_call | solution.py:361
  132.6 0.1 fusion.9
  132.7 2.4 %fusion = f32[16,256,32]{1,2,0:T(8,128)} fusion(f32[8,2,16,256]{3,2,1,0:T(8,128)} %get-tuple-element.5, f32[8,1,32]{2,0,1:T(8,128)S(1)} %get-tuple-element.9, f32[8,1,32]{2,0,1:T(8,128)S(1)} %get-tuple-element.8), kind=kOutput, calls=%fused_computation.1 | convolution fusion | flops 25297408 | bytes 788480 | tf_op jit(solution)/shard_map/frsc,frl->scl/dot_general | solution.py:417
  135.1 7.8 %copy.10 = bf16[1,2,256,8192]{3,2,1,0:T(8,128)(2,1)} copy(bf16[1,2,256,8192]{3,2,1,0:T(8,128)(2,1)} %bitcast.21) | data formatting | bytes 16777216
  (3 shorter events, 0.1 us)
Async XLA Ops:
  0.6 23.6 %copy-start.2 = (s32[256,512]{1,0:T(8,128)S(1)}, s32[256,512]{1,0:T(8,128)}, u32[]{:S(2)}) copy-start(s32[256,512]{1,0:T(8,128)} %param.4) | copy-start | bytes 1572868
  1.8 23.6 %copy-start.1 = (bf16[1,256,1024]{2,1,0:T(8,128)(2,1)S(1)}, bf16[1,256,1024]{2,1,0:T(8,128)(2,1)}, u32[]{:S(2)}) copy-start(bf16[1,256,1024]{2,1,0:T(8,128)(2,1)} %param.3) | copy-start | bytes 1572868
  25.4 1.3 copy-start.3
  25.6 2.0 %copy-start = (bf16[1,256,1024]{2,1,0:T(8,128)(2,1)}, bf16[1,256,1024]{2,1,0:T(8,128)(2,1)S(1)}, u32[]{:S(2)}) copy-start(bf16[1,256,1024]{2,1,0:T(8,128)(2,1)S(1)} %fusion.2) | copy-start | bytes 1572868

commit v7 on v6

--- a/solution.py
+++ b/solution.py
@@ -298,11 +298,22 @@
     send(rows(across, xl), rows(across, xl), recv_ring.at[0, 2], nxt)
     send(held.at[across], held.at[across], recv_sib.at[1], sib)
     compute(across)
-    wait(held.at[sib], recv_sib.at[0], sib)
-    compute(sib)
-    sib_across = blk(z, 1 - xl, 1 - c)
-    wait(held.at[sib_across], recv_sib.at[1], sib)
-    compute(sib_across)
+
+    def finish(t):
+        zo = (z - step * (t + 1) + 2 * zs) % zs
+        part = blk(zo, 1 - xl, c)
+        wait(rows(part, 1 - xl), recv_x.at[1 + t], partner)
+        send(rows(part, 1 - xl), rows(part, 1 - xl), recv_sib.at[2 + 3 * (zs - 1) + t], sib)
+        compute(part)
+        zt = (z + step * (t + 1) + 2 * zs) % zs
+        sfull = blk(zt, xl, 1 - c)
+        spart = blk(zt, 1 - xl, 1 - c)
+        for k, (b, h) in enumerate(((sfull, 0), (sfull, 1), (spart, xl))):
+            wait(rows(b, h), recv_sib.at[2 + 3 * t + k], sib)
+        compute(sfull)
+        wait(rows(spart, 1 - xl), recv_sib.at[2 + 3 * (zs - 1) + t], sib)
+        compute(spart)
+
     for s in range(zs - 1):
         zo = (z - step * (s + 1) + 2 * zs) % zs
         full = blk(zo, xl, c)
@@ -315,17 +326,15 @@
             send(rows(b, h), rows(b, h), recv_sib.at[2 + 3 * s + k], sib)
         send(rows(full, xl), rows(full, xl), recv_x.at[1 + s], partner)
         compute(full)
-        wait(rows(part, 1 - xl), recv_x.at[1 + s], partner)
-        send(rows(part, 1 - xl), rows(part, 1 - xl), recv_sib.at[2 + 3 * (zs - 1) + s], sib)
-        compute(part)
-        zt = (z + step * (s + 1) + 2 * zs) % zs
-        sfull = blk(zt, xl, 1 - c)
-        spart = blk(zt, 1 - xl, 1 - c)
-        for k, (b, h) in enumerate(((sfull, 0), (sfull, 1), (spart, xl))):
-            wait(rows(b, h), recv_sib.at[2 + 3 * s + k], sib)
-        compute(sfull)
-        wait(rows(spart, 1 - xl), recv_sib.at[2 + 3 * (zs - 1) + s], sib)
-        compute(spart)
+        if s == 0:
+            wait(held.at[sib], recv_sib.at[0], sib)
+            compute(sib)
+            sib_across = blk(z, 1 - xl, 1 - c)
+            wait(held.at[sib_across], recv_sib.at[1], sib)
+            compute(sib_across)
+        else:
+            finish(s - 1)
+    finish(zs - 2)
     station = picked[...]
     wide = station.shape[1] // 2
     swapped = jnp.concatenate([station[:, wide:], -station[:, :wide]], axis=1)

time: 143 us -> 134 us (0.937)
  Pallas kernels: 126 us -> 117 us
    pallas_call x1, Pallas kernels: 105 us -> 95.6 us  [grp_cross(): pl.pallas_call(functools.partial(_cross_kernel, zs, bands, scaling), out_...]
where the time goes in v7:
time: 134 us
  Pallas kernels  117 us (87%)
  local copies, waits for them, and re-layouts  7.79 us (6%)
  other arithmetic  5.47 us (4%)
  matrix products  2.43 us (2%)
    pallas_call x1, Pallas kernels, grp_cross(): pl.pallas_call(functools.partial(_cross_kernel, zs, bands, scaling), out_...  95.6 us
    pallas_call x1, Pallas kernels, freq_psum(): pl.pallas_call(functools.partial(_psum_kernel, peers), out_shape=jax.Shap...  21.5 us
    unnamed x9, local copies, waits for them, and re-layouts  7.79 us

profile of v7, /device:TPU:1, one launch (start us, length us, event | category | flops | bytes accessed | tf_op | source)
XLA Modules:
  0.0 133.6 jit_solution(17246772768199012549)
XLA Ops:
  0.6 0.0 copy-start.2
  0.6 1.2 convert_element_type.19
  1.8 0.0 copy-start.1
  1.9 0.9 fusion.4.x_ref
  2.8 21.5 %shard_map.50 = f32[256,512]{1,0:T(8,128)} custom-call(f32[256,512]{1,0:T(8,128)} %fusion.4.x_ref), custom_call_target="tpu_custom_call" | custom-call | tf_op jit(solution)/shard_map/pallas_call | solution.py:91
  24.3 0.0 copy-done.2
  24.3 1.2 convert_multiply_fusion
  25.4 0.0 copy-done.1
  25.4 0.0 copy-start.3
  25.5 0.1 fusion.2
  25.6 0.0 copy-start
  25.7 1.1 maximum_bitcast_fusion.1.left_ref
  26.8 0.0 copy-done.3
  26.8 0.8 fusion.5.sel_ref
  27.6 0.0 copy-done
  27.6 95.6 %shard_map.51 = (bf16[2,256,8192]{2,1,0:T(8,128)(2,1)}, f32[8,2,16,256]{3,2,1,0:T(8,128)}) custom-call(bf16[256,1024]{1,0:T(8,128)(2,1)} %bitcast.20, bf16[512,1024]{1,0:T(8,128)(2,1)} %maximum_bitcast_fusion.1.left_ref, bf16[16,8192]{1,0:T(8,128)(2,1)} %fusion.5.sel_ref), custom_call_target="tpu_custom_call" | custom-call | tf_op jit(solution)/shard_map/pallas_call | solution.py:370
  123.2 0.1 fusion.9
  123.4 2.4 %fusion = f32[16,256,32]{1,2,0:T(8,128)} fusion(f32[8,2,16,256]{3,2,1,0:T(8,128)} %get-tuple-element.5, f32[8,1,32]{2,0,1:T(8,128)S(1)} %get-tuple-element.9, f32[8,1,32]{2,0,1:T(8,128)S(1)} %get-tuple-element.8), kind=kOutput, calls=%fused_computation.1 | convolution fusion | flops 25297408 | bytes 788480 | tf_op jit(solution)/shard_map/frsc,frl->scl/dot_general | solution.py:426
  125.8 7.8 %copy.10 = bf16[1,2,256,8192]{3,2,1,0:T(8,128)(2,1)} copy(bf16[1,2,256,8192]{3,2,1,0:T(8,128)(2,1)} %bitcast.21) | data formatting | bytes 16777216
  (3 shorter events, 0.1 us)
Async XLA Ops:
  0.6 23.6 %copy-start.2 = (s32[256,512]{1,0:T(8,128)S(1)}, s32[256,512]{1,0:T(8,128)}, u32[]{:S(2)}) copy-start(s32[256,512]{1,0:T(8,128)} %param.4) | copy-start | bytes 1572868
  1.8 23.6 %copy-start.1 = (bf16[1,256,1024]{2,1,0:T(8,128)(2,1)S(1)}, bf16[1,256,1024]{2,1,0:T(8,128)(2,1)}, u32[]{:S(2)}) copy-start(bf16[1,256,1024]{2,1,0:T(8,128)(2,1)} %param.3) | copy-start | bytes 1572868
  25.4 1.3 copy-start.3
  25.6 2.0 %copy-start = (bf16[1,256,1024]{2,1,0:T(8,128)(2,1)}, bf16[1,256,1024]{2,1,0:T(8,128)(2,1)S(1)}, u32[]{:S(2)}) copy-start(bf16[1,256,1024]{2,1,0:T(8,128)(2,1)S(1)} %fusion.2) | copy-start | bytes 1572868

commit v8 on v7

--- a/solution.py
+++ b/solution.py
@@ -9,6 +9,7 @@
 from jax.sharding import PartitionSpec as P
 
 LAGS = 256
+SPLIT = 4
 MESH = pl.DeviceIdType.MESH
 
 
@@ -217,7 +218,7 @@
     )(x)
 
 
-def _cross_kernel(zs, bands, scaling, x_ref, left_ref, sel_ref, cross_ref, bins_ref, held, stage, picked,
+def _cross_kernel(zs, split, bands, scaling, x_ref, left_ref, sel_ref, cross_ref, bins_ref, held, stage, picked,
                   send_sem, recv_ring, recv_x, recv_sib, out_sem, recv_f):
     me = lax.axis_index("grp")
     band = lax.axis_index("freq")
@@ -266,6 +267,16 @@
     def rows(b, h):
         return held.at[b, pl.ds(pl.multiple_of(h * half, half), half)]
 
+    piece = width // split
+
+    def bit(b, i):
+        return held.at[b, pl.ds(pl.multiple_of(i * piece, piece), piece)]
+
+    def ring_pieces(full, part, x_of):
+        return [(full, i) for i in range(split)] + [(part, x_of * (split // 2) + j) for j in range(split // 2)]
+
+    count = split + split // 2
+
     def compute(b):
         block = held[b]
         prod = lax.dot_general(
@@ -290,12 +301,14 @@
     held[own] = x_ref[...]
     send(x_ref, held.at[own], recv_x.at[0], partner)
     send(x_ref, held.at[own], recv_sib.at[0], sib)
-    send(x_ref.at[pl.ds(0, half)], rows(own, 0), recv_ring.at[0, 0], nxt)
-    send(x_ref.at[pl.ds(half, half)], rows(own, 1), recv_ring.at[0, 1], nxt)
+    for i in range(split):
+        send(x_ref.at[pl.ds(i * piece, piece)], bit(own, i), recv_ring.at[0, i], nxt)
     compute(own)
     across = blk(z, 1 - xl, c)
     wait(held.at[across], recv_x.at[0], partner)
-    send(rows(across, xl), rows(across, xl), recv_ring.at[0, 2], nxt)
+    for j in range(split // 2):
+        b, i = across, xl * (split // 2) + j
+        send(bit(b, i), bit(b, i), recv_ring.at[0, split + j], nxt)
     send(held.at[across], held.at[across], recv_sib.at[1], sib)
     compute(across)
 
@@ -303,27 +316,26 @@
         zo = (z - step * (t + 1) + 2 * zs) % zs
         part = blk(zo, 1 - xl, c)
         wait(rows(part, 1 - xl), recv_x.at[1 + t], partner)
-        send(rows(part, 1 - xl), rows(part, 1 - xl), recv_sib.at[2 + 3 * (zs - 1) + t], sib)
+        send(rows(part, 1 - xl), rows(part, 1 - xl), recv_sib.at[2 + count * (zs - 1) + t], sib)
         compute(part)
         zt = (z + step * (t + 1) + 2 * zs) % zs
         sfull = blk(zt, xl, 1 - c)
         spart = blk(zt, 1 - xl, 1 - c)
-        for k, (b, h) in enumerate(((sfull, 0), (sfull, 1), (spart, xl))):
-            wait(rows(b, h), recv_sib.at[2 + 3 * t + k], sib)
+        for k, (b, i) in enumerate(ring_pieces(sfull, spart, xl)):
+            wait(bit(b, i), recv_sib.at[2 + count * t + k], sib)
         compute(sfull)
-        wait(rows(spart, 1 - xl), recv_sib.at[2 + 3 * (zs - 1) + t], sib)
+        wait(rows(spart, 1 - xl), recv_sib.at[2 + count * (zs - 1) + t], sib)
         compute(spart)
 
     for s in range(zs - 1):
         zo = (z - step * (s + 1) + 2 * zs) % zs
         full = blk(zo, xl, c)
         part = blk(zo, 1 - xl, c)
-        pieces = ((full, 0), (full, 1), (part, xl))
-        for k, (b, h) in enumerate(pieces):
-            wait(rows(b, h), recv_ring.at[s, k], prv)
+        for k, (b, i) in enumerate(ring_pieces(full, part, xl)):
+            wait(bit(b, i), recv_ring.at[s, k], prv)
             if s < zs - 2:
-                send(rows(b, h), rows(b, h), recv_ring.at[s + 1, k], nxt)
-            send(rows(b, h), rows(b, h), recv_sib.at[2 + 3 * s + k], sib)
+                send(bit(b, i), bit(b, i), recv_ring.at[s + 1, k], nxt)
+            send(bit(b, i), bit(b, i), recv_sib.at[2 + count * s + k], sib)
         send(rows(full, xl), rows(full, xl), recv_x.at[1 + s], partner)
         compute(full)
         if s == 0:
@@ -368,7 +380,7 @@
     bands = lax.axis_size("freq")
     width, cols = whitened.shape
     return pl.pallas_call(
-        functools.partial(_cross_kernel, zs, bands, scaling),
+        functools.partial(_cross_kernel, zs, SPLIT, bands, scaling),
         out_shape=(
             jax.ShapeDtypeStruct((2, width, groups * width), whitened.dtype),
             jax.ShapeDtypeStruct((bands, 2, selector.shape[0], width), jnp.float32),
@@ -379,10 +391,10 @@
             pltpu.VMEM((groups, width, cols), whitened.dtype),
             pltpu.VMEM((2, 2, width, width), whitened.dtype),
             pltpu.VMEM((selector.shape[0], cols), jnp.float32),
-            pltpu.SemaphoreType.DMA((8 * zs + 16,)),
-            pltpu.SemaphoreType.DMA((zs - 1, 3)),
+            pltpu.SemaphoreType.DMA((4 * SPLIT * zs + 16,)),
+            pltpu.SemaphoreType.DMA((zs - 1, SPLIT + SPLIT // 2)),
             pltpu.SemaphoreType.DMA((zs,)),
-            pltpu.SemaphoreType.DMA((2 + 4 * (zs - 1),)),
+            pltpu.SemaphoreType.DMA((2 + (SPLIT + SPLIT // 2 + 1) * (zs - 1),)),
             pltpu.SemaphoreType.DMA((2,)),
             pltpu.SemaphoreType.DMA((bands,)),
         ],

time: 134 us -> 135 us (level)
  no operation moved by 1% of the time
where the time goes in v8:
time: 135 us
  Pallas kernels  118 us (87%)
  local copies, waits for them, and re-layouts  7.79 us (6%)
  other arithmetic  5.47 us (4%)
  matrix products  2.43 us (2%)
    pallas_call x1, Pallas kernels, grp_cross(): pl.pallas_call(functools.partial(_cross_kernel, zs, SPLIT, bands, scaling...  96.6 us
    pallas_call x1, Pallas kernels, freq_psum(): pl.pallas_call(functools.partial(_psum_kernel, peers), out_shape=jax.Shap...  21.5 us
    unnamed x9, local copies, waits for them, and re-layouts  7.79 us

profile of v8, /device:TPU:1, one launch (start us, length us, event | category | flops | bytes accessed | tf_op | source)
XLA Modules:
  0.0 134.6 jit_solution(17936641668452132907)
XLA Ops:
  0.6 0.0 copy-start.2
  0.6 1.2 convert_element_type.19
  1.8 0.0 copy-start.1
  1.9 0.9 fusion.4.x_ref
  2.8 21.5 %shard_map.50 = f32[256,512]{1,0:T(8,128)} custom-call(f32[256,512]{1,0:T(8,128)} %fusion.4.x_ref), custom_call_target="tpu_custom_call" | custom-call | tf_op jit(solution)/shard_map/pallas_call | solution.py:92
  24.3 0.0 copy-done.2
  24.3 1.2 convert_multiply_fusion
  25.4 0.0 copy-done.1
  25.4 0.0 copy-start.3
  25.5 0.1 fusion.2
  25.6 0.0 copy-start
  25.7 1.1 maximum_bitcast_fusion.1.left_ref
  26.8 0.0 copy-done.3
  26.8 0.8 fusion.5.sel_ref
  27.6 0.0 copy-done
  27.6 96.6 %shard_map.51 = (bf16[2,256,8192]{2,1,0:T(8,128)(2,1)}, f32[8,2,16,256]{3,2,1,0:T(8,128)}) custom-call(bf16[256,1024]{1,0:T(8,128)(2,1)} %bitcast.20, bf16[512,1024]{1,0:T(8,128)(2,1)} %maximum_bitcast_fusion.1.left_ref, bf16[16,8192]{1,0:T(8,128)(2,1)} %fusion.5.sel_ref), custom_call_target="tpu_custom_call" | custom-call | tf_op jit(solution)/shard_map/pallas_call | solution.py:382
  124.3 0.1 fusion.9
  124.4 2.4 %fusion = f32[16,256,32]{1,2,0:T(8,128)} fusion(f32[8,2,16,256]{3,2,1,0:T(8,128)} %get-tuple-element.5, f32[8,1,32]{2,0,1:T(8,128)S(1)} %get-tuple-element.9, f32[8,1,32]{2,0,1:T(8,128)S(1)} %get-tuple-element.8), kind=kOutput, calls=%fused_computation.1 | convolution fusion | flops 25297408 | bytes 788480 | tf_op jit(solution)/shard_map/frsc,frl->scl/dot_general | solution.py:438
  126.8 7.8 %copy.10 = bf16[1,2,256,8192]{3,2,1,0:T(8,128)(2,1)} copy(bf16[1,2,256,8192]{3,2,1,0:T(8,128)(2,1)} %bitcast.21) | data formatting | bytes 16777216
  (3 shorter events, 0.1 us)
Async XLA Ops:
  0.6 23.6 %copy-start.2 = (s32[256,512]{1,0:T(8,128)S(1)}, s32[256,512]{1,0:T(8,128)}, u32[]{:S(2)}) copy-start(s32[256,512]{1,0:T(8,128)} %param.4) | copy-start | bytes 1572868
  1.8 23.6 %copy-start.1 = (bf16[1,256,1024]{2,1,0:T(8,128)(2,1)S(1)}, bf16[1,256,1024]{2,1,0:T(8,128)(2,1)}, u32[]{:S(2)}) copy-start(bf16[1,256,1024]{2,1,0:T(8,128)(2,1)} %param.3) | copy-start | bytes 1572868
  25.4 1.3 copy-start.3
  25.6 2.0 %copy-start = (bf16[1,256,1024]{2,1,0:T(8,128)(2,1)}, bf16[1,256,1024]{2,1,0:T(8,128)(2,1)S(1)}, u32[]{:S(2)}) copy-start(bf16[1,256,1024]{2,1,0:T(8,128)(2,1)S(1)} %fusion.2) | copy-start | bytes 1572868

commit v9 on v7

--- a/solution.py
+++ b/solution.py
@@ -217,8 +217,8 @@
     )(x)
 
 
-def _cross_kernel(zs, bands, scaling, x_ref, left_ref, sel_ref, cross_ref, bins_ref, held, stage, picked,
-                  send_sem, recv_ring, recv_x, recv_sib, out_sem, recv_f):
+def _cross_kernel(zs, bands, scaling, x_ref, left_ref, sel_ref, cross_ref, bins_ref, held, picked,
+                  send_sem, recv_ring, recv_x, recv_sib, recv_f):
     me = lax.axis_index("grp")
     band = lax.axis_index("freq")
     c = me % 2
@@ -247,7 +247,6 @@
     pl.semaphore_wait(barrier, 4 + bands - 1)
 
     sends = []
-    outs = []
 
     def send(src, dst, recv, g):
         copy = pltpu.make_async_remote_copy(
@@ -271,15 +270,9 @@
         prod = lax.dot_general(
             left_ref[...], block, (((1,), (1,)), ((), ())), preferred_element_type=jnp.float32
         )
-        slot = len(outs) % 2
-        if len(outs) >= 2:
-            outs[-2].wait()
-        stage[slot] = (prod * scaling).astype(stage.dtype).reshape(stage.shape[1:])
-        copy = pltpu.make_async_copy(
-            stage.at[slot], cross_ref.at[:, :, pl.ds(pl.multiple_of(b * width, width), width)], out_sem.at[slot]
-        )
-        copy.start()
-        outs.append(copy)
+        cross_ref[:, :, pl.ds(pl.multiple_of(b * width, width), width)] = (
+            (prod * scaling).astype(cross_ref.dtype).reshape(2, width, width)
+        )
         picked[...] += jnp.dot(
             sel_ref[:, pl.ds(pl.multiple_of(b * width, width), width)], block,
             preferred_element_type=jnp.float32,
@@ -357,8 +350,6 @@
             src_ref=bins_ref.at[src], dst_ref=bins_ref.at[src], send_sem=send_sem.at[0],
             recv_sem=recv_f.at[src], device_id=(me, src), device_id_type=MESH,
         ).wait_recv()
-    for copy in outs[-2:]:
-        copy.wait()
     for copy in sends:
         copy.wait_send()
 
@@ -374,16 +365,14 @@
             jax.ShapeDtypeStruct((bands, 2, selector.shape[0], width), jnp.float32),
         ),
         in_specs=[pl.BlockSpec(memory_space=pltpu.VMEM)] * 3,
-        out_specs=(pl.BlockSpec(memory_space=pl.ANY), pl.BlockSpec(memory_space=pltpu.VMEM)),
+        out_specs=(pl.BlockSpec(memory_space=pltpu.VMEM), pl.BlockSpec(memory_space=pltpu.VMEM)),
         scratch_shapes=[
             pltpu.VMEM((groups, width, cols), whitened.dtype),
-            pltpu.VMEM((2, 2, width, width), whitened.dtype),
             pltpu.VMEM((selector.shape[0], cols), jnp.float32),
             pltpu.SemaphoreType.DMA((8 * zs + 16,)),
             pltpu.SemaphoreType.DMA((zs - 1, 3)),
             pltpu.SemaphoreType.DMA((zs,)),
             pltpu.SemaphoreType.DMA((2 + 4 * (zs - 1),)),
-            pltpu.SemaphoreType.DMA((2,)),
             pltpu.SemaphoreType.DMA((bands,)),
         ],
         compiler_params=pltpu.CompilerParams(

time: 134 us -> 136 us (1.015)
  Pallas kernels: 117 us -> 120 us
    pallas_call x1, Pallas kernels: 95.6 us -> 98.2 us  [grp_cross(): pl.pallas_call(functools.partial(_cross_kernel, zs, bands, scaling), out_...]
where the time goes in v9:
time: 136 us
  Pallas kernels  120 us (88%)
  local copies, waits for them, and re-layouts  7.79 us (6%)
  other arithmetic  5.47 us (4%)
  matrix products  2.43 us (2%)
    pallas_call x1, Pallas kernels, grp_cross(): pl.pallas_call(functools.partial(_cross_kernel, zs, bands, scaling), out_...  98.2 us
    pallas_call x1, Pallas kernels, freq_psum(): pl.pallas_call(functools.partial(_psum_kernel, peers), out_shape=jax.Shap...  21.5 us
    unnamed x9, local copies, waits for them, and re-layouts  7.79 us

profile of v9, /device:TPU:1, one launch (start us, length us, event | category | flops | bytes accessed | tf_op | source)
XLA Modules:
  0.0 136.2 jit_solution(3395659557488652440)
XLA Ops:
  0.6 0.0 copy-start.2
  0.6 1.2 convert_element_type.19
  1.8 0.0 copy-start.1
  1.9 0.9 fusion.4.x_ref
  2.8 21.5 %shard_map.50 = f32[256,512]{1,0:T(8,128)} custom-call(f32[256,512]{1,0:T(8,128)} %fusion.4.x_ref), custom_call_target="tpu_custom_call" | custom-call | tf_op jit(solution)/shard_map/pallas_call | solution.py:91
  24.3 0.0 copy-done.2
  24.3 1.2 convert_multiply_fusion
  25.4 0.0 copy-done.1
  25.4 0.0 copy-start.3
  25.5 0.1 fusion.2
  25.6 0.0 copy-start
  25.7 1.1 maximum_bitcast_fusion.1.left_ref
  26.8 0.0 copy-done.3
  26.8 0.8 fusion.5.sel_ref
  27.6 0.0 copy-done
  27.6 98.2 %shard_map.51 = (bf16[2,256,8192]{2,1,0:T(8,128)(2,1)}, f32[8,2,16,256]{3,2,1,0:T(8,128)}) custom-call(bf16[256,1024]{1,0:T(8,128)(2,1)} %bitcast.20, bf16[512,1024]{1,0:T(8,128)(2,1)} %maximum_bitcast_fusion.1.left_ref, bf16[16,8192]{1,0:T(8,128)(2,1)} %fusion.5.sel_ref), custom_call_target="tpu_custom_call" | custom-call | tf_op jit(solution)/shard_map/pallas_call | solution.py:361
  125.9 0.1 fusion.9
  126.0 2.4 %fusion = f32[16,256,32]{1,2,0:T(8,128)} fusion(f32[8,2,16,256]{3,2,1,0:T(8,128)} %get-tuple-element.5, f32[8,1,32]{2,0,1:T(8,128)S(1)} %get-tuple-element.9, f32[8,1,32]{2,0,1:T(8,128)S(1)} %get-tuple-element.8), kind=kOutput, calls=%fused_computation.1 | convolution fusion | flops 25297408 | bytes 788480 | tf_op jit(solution)/shard_map/frsc,frl->scl/dot_general | solution.py:415
  128.4 7.8 %copy.10 = bf16[1,2,256,8192]{3,2,1,0:T(8,128)(2,1)} copy(bf16[1,2,256,8192]{3,2,1,0:T(8,128)(2,1)} %bitcast.21) | data formatting | bytes 16777216
  (3 shorter events, 0.1 us)
Async XLA Ops:
  0.6 23.6 %copy-start.2 = (s32[256,512]{1,0:T(8,128)S(1)}, s32[256,512]{1,0:T(8,128)}, u32[]{:S(2)}) copy-start(s32[256,512]{1,0:T(8,128)} %param.4) | copy-start | bytes 1572868
  1.8 23.6 %copy-start.1 = (bf16[1,256,1024]{2,1,0:T(8,128)(2,1)S(1)}, bf16[1,256,1024]{2,1,0:T(8,128)(2,1)}, u32[]{:S(2)}) copy-start(bf16[1,256,1024]{2,1,0:T(8,128)(2,1)} %param.3) | copy-start | bytes 1572868
  25.4 1.3 copy-start.3
  25.6 2.0 %copy-start = (bf16[1,256,1024]{2,1,0:T(8,128)(2,1)}, bf16[1,256,1024]{2,1,0:T(8,128)(2,1)S(1)}, u32[]{:S(2)}) copy-start(bf16[1,256,1024]{2,1,0:T(8,128)(2,1)S(1)} %fusion.2) | copy-start | bytes 1572868

commit v10 on v7

--- a/solution.py
+++ b/solution.py
@@ -19,14 +19,20 @@
     pl.semaphore_wait(barrier, peers - 1)
 
 
-def _psum_kernel(peers, x_ref, out_ref, parts, send_a, recv_a, send_b, recv_b):
+def _whiten_kernel(peers, spec_ref, valid_ref, white_ref, left_ref, x_ref, out_ref, parts,
+                   send_a, recv_a, send_b, recv_b):
     me = lax.axis_index("freq")
     grp = lax.axis_index("grp")
     rows = x_ref.shape[0] // peers
+    wide = x_ref.shape[1]
 
     def here(peer):
         return (grp, peer)
 
+    spectrum = spec_ref[...].astype(jnp.float32)
+    real_part = spectrum[:, :wide]
+    imag_part = spectrum[:, wide:]
+    x_ref[...] = real_part * real_part + imag_part * imag_part
     _greet(peers, here)
     scatter = []
     for k in range(1, peers):
@@ -84,24 +90,37 @@
         ).wait_recv()
     for copy in gather:
         copy.wait_send()
-
-
-def freq_psum(x, peers):
-    rows, cols = x.shape
+    factor = lax.rsqrt(out_ref[...] / peers + 1e-05)
+    factor = factor * valid_ref[...].astype(jnp.float32)
+    white = (spectrum * jnp.concatenate([factor, factor], axis=1)).astype(white_ref.dtype)
+    white_ref[...] = white
+    count = white.shape[0]
+    left_ref[pl.ds(0, count), :] = white
+    left_ref[pl.ds(count, count), :] = jnp.concatenate([white[:, wide:], -white[:, :wide]], axis=1)
+
+
+def freq_whiten(spectra, valid, peers):
+    chans, double_width = spectra.shape
+    wide = double_width // 2
     return pl.pallas_call(
-        functools.partial(_psum_kernel, peers),
-        out_shape=jax.ShapeDtypeStruct((rows, cols), x.dtype),
-        in_specs=[pl.BlockSpec(memory_space=pltpu.VMEM)],
-        out_specs=pl.BlockSpec(memory_space=pltpu.VMEM),
+        functools.partial(_whiten_kernel, peers),
+        out_shape=(
+            jax.ShapeDtypeStruct((chans, double_width), spectra.dtype),
+            jax.ShapeDtypeStruct((2 * chans, double_width), spectra.dtype),
+        ),
+        in_specs=[pl.BlockSpec(memory_space=pltpu.VMEM)] * 2,
+        out_specs=(pl.BlockSpec(memory_space=pltpu.VMEM), pl.BlockSpec(memory_space=pltpu.VMEM)),
         scratch_shapes=[
-            pltpu.VMEM((peers, rows // peers, cols), x.dtype),
+            pltpu.VMEM((chans, wide), jnp.float32),
+            pltpu.VMEM((chans, wide), jnp.float32),
+            pltpu.VMEM((peers, chans // peers, wide), jnp.float32),
             pltpu.SemaphoreType.DMA((peers,)),
             pltpu.SemaphoreType.DMA((peers,)),
             pltpu.SemaphoreType.DMA((peers,)),
             pltpu.SemaphoreType.DMA((peers,)),
         ],
         compiler_params=pltpu.CompilerParams(collective_id=0, has_side_effects=True),
-    )(x)
+    )(spectra, valid)
 
 
 def _gather_kernel(peers, x_ref, out_ref, send_sem, recv_sem):
@@ -396,16 +415,8 @@
     bin_count, chan_count, double_width = spectra.shape
     window_count = double_width // 2
     freq_count = lax.axis_size("freq")
-    spectrum_f32 = spectra.astype(jnp.float32)
-    real_part = spectrum_f32[..., :window_count]
-    imag_part = spectrum_f32[..., window_count:]
-    local_power = jnp.sum(real_part * real_part + imag_part * imag_part, axis=0)
-    band_power = freq_psum(local_power, freq_count)
     total_bins = bin_count * freq_count
-    factor = lax.rsqrt(band_power / total_bins + 1e-05) * valid.astype(jnp.float32)
-    whitened = (spectrum_f32 * jnp.concatenate([factor, factor], axis=1)[None]).astype(jnp.bfloat16)
-    swapped = jnp.concatenate([whitened[..., window_count:], -whitened[..., :window_count]], axis=2)
-    stacked = jnp.concatenate([whitened, swapped], axis=1)
+    white, left = freq_whiten(spectra[0], valid, freq_count)
     scaling = 1.0 / math.sqrt(window_count)
     station_count = station_index.shape[0]
     total_chans = lax.axis_size("grp") * chan_count
@@ -413,7 +424,7 @@
         jnp.bfloat16
     )
     cross, all_bins = grp_cross(
-        whitened[0], stacked[0], selector, scaling, lax.axis_size("grp") // 4
+        white, left, selector, scaling, lax.axis_size("grp") // 4
     )
     cross = cross[None]
 

time: 134 us -> 131 us (0.978)
  other arithmetic: 5.47 us -> 1.6 us
    unnamed x9 -> x1, local copies, waits for them, and re-layouts: 7.79 us -> 7.77 us
where the time goes in v10:
time: 131 us
  Pallas kernels  118 us (90%)
  local copies, waits for them, and re-layouts  7.77 us (6%)
  matrix products  2.43 us (2%)
  other arithmetic  1.6 us (1%)
    pallas_call x1, Pallas kernels, grp_cross(): pl.pallas_call(functools.partial(_cross_kernel, zs, bands, scaling), out_...  95.6 us
    pallas_call x1, Pallas kernels, freq_whiten(): pl.pallas_call(functools.partial(_whiten_kernel, peers), out_shape=(jax.S...  22.6 us
    unnamed x1, local copies, waits for them, and re-layouts  7.77 us

profile of v10, /device:TPU:1, one launch (start us, length us, event | category | flops | bytes accessed | tf_op | source)
XLA Modules:
  0.0 130.7 jit_solution(7346169850766822804)
XLA Ops:
  0.6 22.6 %shard_map.50 = (bf16[256,1024]{1,0:T(8,128)(2,1)}, bf16[512,1024]{1,0:T(8,128)(2,1)}) custom-call(bf16[256,1024]{1,0:T(8,128)(2,1)} %bitcast.11, s32[256,512]{1,0:T(8,128)} %valid_ref.1), custom_call_target="tpu_custom_call" | custom-call | tf_op jit(solution)/shard_map/pallas_call | solution.py:105
  23.2 1.5 %fusion.1.sel_ref = bf16[16,8192]{1,0:T(8,128)(2,1)} fusion(s32[16]{0:T(128)} %param.5), kind=kLoop, calls=%fused_computation.3 | loop fusion | flops 262144 | bytes 262208 | tf_op jit(solution)/shard_map/convert_element_type | solution.py:423
  24.7 95.6 %shard_map.51 = (bf16[2,256,8192]{2,1,0:T(8,128)(2,1)}, f32[8,2,16,256]{3,2,1,0:T(8,128)}) custom-call(bf16[256,1024]{1,0:T(8,128)(2,1)} %get-tuple-element.6.x_ref, bf16[512,1024]{1,0:T(8,128)(2,1)} %get-tuple-element.7.left_ref, bf16[16,8192]{1,0:T(8,128)(2,1)} %fusion.1.sel_ref), custom_call_target="tpu_custom_call" | custom-call | tf_op jit(solution)/shard_map/pallas_call | solution.py:389
  120.3 0.1 fusion.5
  120.5 2.4 %fusion = f32[16,256,32]{1,2,0:T(8,128)} fusion(f32[8,2,16,256]{3,2,1,0:T(8,128)} %get-tuple-element.9, f32[8,1,32]{2,0,1:T(8,128)S(1)} %get-tuple-element.11, f32[8,1,32]{2,0,1:T(8,128)S(1)} %get-tuple-element.10), kind=kOutput, calls=%fused_computation.1 | convolution fusion | flops 25297408 | bytes 788480 | tf_op jit(solution)/shard_map/frsc,frl->scl/dot_general | solution.py:437
  122.9 7.8 %copy.10 = bf16[1,2,256,8192]{3,2,1,0:T(8,128)(2,1)} copy(bf16[1,2,256,8192]{3,2,1,0:T(8,128)(2,1)} %bitcast.10) | data formatting | bytes 16777216
  (2 shorter events, 0.0 us)

commit v11 on v10

--- a/solution.py
+++ b/solution.py
@@ -299,10 +299,9 @@
         )
         copy.start()
         outs.append(copy)
-        picked[...] += jnp.dot(
-            sel_ref[:, pl.ds(pl.multiple_of(b * width, width), width)], block,
-            preferred_element_type=jnp.float32,
-        )
+        columns = b * width + lax.broadcasted_iota(jnp.int32, (sel_ref.shape[0], width), 1)
+        chosen = (sel_ref[...] == columns).astype(block.dtype)
+        picked[...] += jnp.dot(chosen, block, preferred_element_type=jnp.float32)
 
     picked[...] = jnp.zeros_like(picked)
     own = blk(z, xl, c)
@@ -419,10 +418,7 @@
     white, left = freq_whiten(spectra[0], valid, freq_count)
     scaling = 1.0 / math.sqrt(window_count)
     station_count = station_index.shape[0]
-    total_chans = lax.axis_size("grp") * chan_count
-    selector = (station_index[:, None] == jnp.arange(total_chans, dtype=jnp.int32)[None, :]).astype(
-        jnp.bfloat16
-    )
+    selector = station_index[:, None]
     cross, all_bins = grp_cross(
         white, left, selector, scaling, lax.axis_size("grp") // 4
     )

time: 131 us -> 131 us (level)
  other arithmetic: 1.6 us -> 0.12 us
  local copies, waits for them, and re-layouts: 7.77 us -> 9.1 us
    convert_element_type x1 -> x0, other arithmetic: 1.47 us -> none  [on_device(): (station_index[:, None] == jnp.arange(total_chans, dtype=jnp.int32)[None,...]
    broadcast_in_dim x0 -> x1, local copies, waits for them, and re-layouts: none -> 1.33 us  [on_device(): selector = station_index[:, None]]
where the time goes in v11:
time: 131 us; the launch traced here: 130 us
  Pallas kernels  118 us (90%)
  local copies, waits for them, and re-layouts  9.1 us (7%)
  matrix products  2.43 us (2%)
    pallas_call x1, Pallas kernels, grp_cross(): pl.pallas_call(functools.partial(_cross_kernel, zs, bands, scaling), out_...  95.6 us
    pallas_call x1, Pallas kernels, freq_whiten(): pl.pallas_call(functools.partial(_whiten_kernel, peers), out_shape=(jax.S...  22.6 us
    unnamed x1, local copies, waits for them, and re-layouts  7.77 us

profile of v11, /device:TPU:1, one launch (start us, length us, event | category | flops | bytes accessed | tf_op | source)
XLA Modules:
  0.0 130.5 jit_solution(15324529482437120563)
XLA Ops:
  0.6 22.6 %shard_map.50 = (bf16[256,1024]{1,0:T(8,128)(2,1)}, bf16[512,1024]{1,0:T(8,128)(2,1)}) custom-call(bf16[256,1024]{1,0:T(8,128)(2,1)} %bitcast.12, s32[256,512]{1,0:T(8,128)} %valid_ref.1), custom_call_target="tpu_custom_call" | custom-call | tf_op jit(solution)/shard_map/pallas_call | solution.py:105
  23.2 1.3 %copy.5.sel_ref = s32[16,1]{1,0:T(8,128)} copy(s32[16,1]{0,1:T(1,128)} %bitcast.13) | data formatting | bytes 128 | tf_op jit(solution)/shard_map/broadcast_in_dim | solution.py:421
  24.5 95.6 %shard_map.51 = (bf16[2,256,8192]{2,1,0:T(8,128)(2,1)}, f32[8,2,16,256]{3,2,1,0:T(8,128)}) custom-call(bf16[256,1024]{1,0:T(8,128)(2,1)} %get-tuple-element.6.x_ref, bf16[512,1024]{1,0:T(8,128)(2,1)} %get-tuple-element.7.left_ref, s32[16,1]{1,0:T(8,128)} %copy.5.sel_ref), custom_call_target="tpu_custom_call" | custom-call | tf_op jit(solution)/shard_map/pallas_call | solution.py:388
  120.1 0.1 fusion.4
  120.3 2.4 %fusion = f32[16,256,32]{1,2,0:T(8,128)} fusion(f32[8,2,16,256]{3,2,1,0:T(8,128)} %get-tuple-element.9, f32[8,1,32]{2,0,1:T(8,128)S(1)} %get-tuple-element.11, f32[8,1,32]{2,0,1:T(8,128)S(1)} %get-tuple-element.10), kind=kOutput, calls=%fused_computation.1 | convolution fusion | flops 25297408 | bytes 788480 | tf_op jit(solution)/shard_map/frsc,frl->scl/dot_general | solution.py:433
  122.7 7.8 %copy.11 = bf16[1,2,256,8192]{3,2,1,0:T(8,128)(2,1)} copy(bf16[1,2,256,8192]{3,2,1,0:T(8,128)(2,1)} %bitcast.11) | data formatting | bytes 16777216
  (2 shorter events, 0.0 us)

commit v12 on v11

--- a/solution.py
+++ b/solution.py
@@ -299,11 +299,16 @@
         )
         copy.start()
         outs.append(copy)
-        columns = b * width + lax.broadcasted_iota(jnp.int32, (sel_ref.shape[0], width), 1)
-        chosen = (sel_ref[...] == columns).astype(block.dtype)
+        columns = b * width + lax.broadcasted_iota(jnp.int32, (stations, width), 1)
+        chosen = (station_ids == columns).astype(block.dtype)
         picked[...] += jnp.dot(chosen, block, preferred_element_type=jnp.float32)
 
     picked[...] = jnp.zeros_like(picked)
+    stations = picked.shape[0]
+    place = lax.broadcasted_iota(jnp.int32, (stations, width), 0)
+    station_ids = jnp.zeros((stations, width), jnp.int32)
+    for k in range(stations):
+        station_ids = jnp.where(place == k, sel_ref[k], station_ids)
     own = blk(z, xl, c)
     held[own] = x_ref[...]
     send(x_ref, held.at[own], recv_x.at[0], partner)
@@ -391,7 +396,7 @@
             jax.ShapeDtypeStruct((2, width, groups * width), whitened.dtype),
             jax.ShapeDtypeStruct((bands, 2, selector.shape[0], width), jnp.float32),
         ),
-        in_specs=[pl.BlockSpec(memory_space=pltpu.VMEM)] * 3,
+        in_specs=[pl.BlockSpec(memory_space=pltpu.VMEM)] * 2 + [pl.BlockSpec(memory_space=pltpu.SMEM)],
         out_specs=(pl.BlockSpec(memory_space=pl.ANY), pl.BlockSpec(memory_space=pltpu.VMEM)),
         scratch_shapes=[
             pltpu.VMEM((groups, width, cols), whitened.dtype),
@@ -418,7 +423,7 @@
     white, left = freq_whiten(spectra[0], valid, freq_count)
     scaling = 1.0 / math.sqrt(window_count)
     station_count = station_index.shape[0]
-    selector = station_index[:, None]
+    selector = station_index
     cross, all_bins = grp_cross(
         white, left, selector, scaling, lax.axis_size("grp") // 4
     )

time: 131 us -> 130 us (level)
  local copies, waits for them, and re-layouts: 9.1 us -> 7.77 us
    broadcast_in_dim x1 -> x0, local copies, waits for them, and re-layouts: 1.33 us -> none  [on_device(): selector = station_index[:, None]]
where the time goes in v12:
time: 130 us; the launch traced here: 129 us
  Pallas kernels  118 us (91%)
  local copies, waits for them, and re-layouts  7.77 us (6%)
  matrix products  2.43 us (2%)
    pallas_call x1, Pallas kernels, grp_cross(): pl.pallas_call(functools.partial(_cross_kernel, zs, bands, scaling), out_...  95.8 us
    pallas_call x1, Pallas kernels, freq_whiten(): pl.pallas_call(functools.partial(_whiten_kernel, peers), out_shape=(jax.S...  22.6 us
    unnamed x1, local copies, waits for them, and re-layouts  7.77 us

profile of v12, /device:TPU:1, one launch (start us, length us, event | category | flops | bytes accessed | tf_op | source)
XLA Modules:
  0.0 129.3 jit_solution(5029900662965316592)
XLA Ops:
  0.6 22.6 %shard_map.50 = (bf16[256,1024]{1,0:T(8,128)(2,1)}, bf16[512,1024]{1,0:T(8,128)(2,1)}) custom-call(bf16[256,1024]{1,0:T(8,128)(2,1)} %bitcast.11, s32[256,512]{1,0:T(8,128)} %valid_ref.1), custom_call_target="tpu_custom_call" | custom-call | tf_op jit(solution)/shard_map/pallas_call | solution.py:105
  23.2 95.8 %shard_map.51 = (bf16[2,256,8192]{2,1,0:T(8,128)(2,1)}, f32[8,2,16,256]{3,2,1,0:T(8,128)}) custom-call(bf16[256,1024]{1,0:T(8,128)(2,1)} %get-tuple-element.6.x_ref, bf16[512,1024]{1,0:T(8,128)(2,1)} %get-tuple-element.7.left_ref, s32[16]{0:T(128)} %sel_ref.1), custom_call_target="tpu_custom_call" | custom-call | tf_op jit(solution)/shard_map/pallas_call | solution.py:393
  119.0 0.1 fusion.4
  119.1 2.4 %fusion = f32[16,256,32]{1,2,0:T(8,128)} fusion(f32[8,2,16,256]{3,2,1,0:T(8,128)} %get-tuple-element.9, f32[8,1,32]{2,0,1:T(8,128)S(1)} %get-tuple-element.11, f32[8,1,32]{2,0,1:T(8,128)S(1)} %get-tuple-element.10), kind=kOutput, calls=%fused_computation.1 | convolution fusion | flops 25297408 | bytes 788480 | tf_op jit(solution)/shard_map/frsc,frl->scl/dot_general | solution.py:438
  121.6 7.8 %copy.10 = bf16[1,2,256,8192]{3,2,1,0:T(8,128)(2,1)} copy(bf16[1,2,256,8192]{3,2,1,0:T(8,128)(2,1)} %bitcast.10) | data formatting | bytes 16777216
  (2 shorter events, 0.0 us)

commit v13 on v12

--- a/solution.py
+++ b/solution.py
@@ -19,7 +19,7 @@
     pl.semaphore_wait(barrier, peers - 1)
 
 
-def _whiten_kernel(peers, spec_ref, valid_ref, white_ref, left_ref, x_ref, out_ref, parts,
+def _whiten_kernel(peers, greet, spec_ref, valid_ref, white_ref, left_ref, x_ref, out_ref, parts,
                    send_a, recv_a, send_b, recv_b):
     me = lax.axis_index("freq")
     grp = lax.axis_index("grp")
@@ -33,7 +33,8 @@
     real_part = spectrum[:, :wide]
     imag_part = spectrum[:, wide:]
     x_ref[...] = real_part * real_part + imag_part * imag_part
-    _greet(peers, here)
+    if greet:
+        _greet(peers, here)
     scatter = []
     for k in range(1, peers):
         peer = (me + k) % peers
@@ -103,7 +104,7 @@
     chans, double_width = spectra.shape
     wide = double_width // 2
     return pl.pallas_call(
-        functools.partial(_whiten_kernel, peers),
+        functools.partial(_whiten_kernel, peers, True),
         out_shape=(
             jax.ShapeDtypeStruct((chans, double_width), spectra.dtype),
             jax.ShapeDtypeStruct((2 * chans, double_width), spectra.dtype),
@@ -236,8 +237,9 @@
     )(x)
 
 
-def _cross_kernel(zs, bands, scaling, x_ref, left_ref, sel_ref, cross_ref, bins_ref, held, stage, picked,
-                  send_sem, recv_ring, recv_x, recv_sib, out_sem, recv_f):
+def _cross_kernel(zs, bands, scaling, spec_ref, valid_ref, sel_ref, cross_ref, bins_ref, held, stage, picked,
+                  send_sem, recv_ring, recv_x, recv_sib, out_sem, recv_f, x_ref, left_ref, power, summed, parts,
+                  send_a, recv_a, send_b, recv_b):
     me = lax.axis_index("grp")
     band = lax.axis_index("freq")
     c = me % 2
@@ -264,6 +266,8 @@
     for k in range(1, bands):
         pl.semaphore_signal(barrier, inc=1, device_id=(me, (band + k) % bands), device_id_type=MESH)
     pl.semaphore_wait(barrier, 4 + bands - 1)
+    _whiten_kernel(bands, False, spec_ref, valid_ref, x_ref, left_ref, power, summed, parts,
+                   send_a, recv_a, send_b, recv_b)
 
     sends = []
     outs = []
@@ -386,10 +390,12 @@
         copy.wait_send()
 
 
-def grp_cross(whitened, left, selector, scaling, zs):
+def grp_cross(spectra, valid, selector, scaling, zs):
     groups = lax.axis_size("grp")
     bands = lax.axis_size("freq")
-    width, cols = whitened.shape
+    width, cols = spectra.shape
+    whitened = spectra
+    wide = cols // 2
     return pl.pallas_call(
         functools.partial(_cross_kernel, zs, bands, scaling),
         out_shape=(
@@ -408,11 +414,20 @@
             pltpu.SemaphoreType.DMA((2 + 4 * (zs - 1),)),
             pltpu.SemaphoreType.DMA((2,)),
             pltpu.SemaphoreType.DMA((bands,)),
+            pltpu.VMEM((width, cols), spectra.dtype),
+            pltpu.VMEM((2 * width, cols), spectra.dtype),
+            pltpu.VMEM((width, wide), jnp.float32),
+            pltpu.VMEM((width, wide), jnp.float32),
+            pltpu.VMEM((bands, width // bands, wide), jnp.float32),
+            pltpu.SemaphoreType.DMA((bands,)),
+            pltpu.SemaphoreType.DMA((bands,)),
+            pltpu.SemaphoreType.DMA((bands,)),
+            pltpu.SemaphoreType.DMA((bands,)),
         ],
         compiler_params=pltpu.CompilerParams(
             collective_id=3, has_side_effects=True, vmem_limit_bytes=56 * 1024 * 1024
         ),
-    )(whitened, left, selector)
+    )(spectra, valid, selector)
 
 
 def on_device(spectra, valid, station_index):
@@ -420,12 +435,11 @@
     window_count = double_width // 2
     freq_count = lax.axis_size("freq")
     total_bins = bin_count * freq_count
-    white, left = freq_whiten(spectra[0], valid, freq_count)
     scaling = 1.0 / math.sqrt(window_count)
     station_count = station_index.shape[0]
     selector = station_index
     cross, all_bins = grp_cross(
-        white, left, selector, scaling, lax.axis_size("grp") // 4
+        spectra[0], valid, selector, scaling, lax.axis_size("grp") // 4
     )
     cross = cross[None]
 

time: 130 us -> 124 us (0.954)
  Pallas kernels: 118 us -> 113 us
    pallas_call x1 -> x0, Pallas kernels: 22.6 us -> none  [freq_whiten(): pl.pallas_call(functools.partial(_whiten_kernel, peers), out_shape=(jax.S...]
    pallas_call x1, Pallas kernels: 95.8 us -> 113 us  [grp_cross(): pl.pallas_call(functools.partial(_cross_kernel, zs, bands, scaling), out_...]
where the time goes in v13:
time: 124 us
  Pallas kernels  113 us (91%)
  local copies, waits for them, and re-layouts  7.77 us (6%)
  matrix products  2.43 us (2%)
    pallas_call x1, Pallas kernels, grp_cross(): pl.pallas_call(functools.partial(_cross_kernel, zs, bands, scaling), out_...  113 us
    unnamed x1, local copies, waits for them, and re-layouts  7.77 us

profile of v13, /device:TPU:1, one launch (start us, length us, event | category | flops | bytes accessed | tf_op | source)
XLA Modules:
  0.0 123.9 jit_solution(5336053160153564113)
XLA Ops:
  0.6 113.0 %shard_map.50 = (bf16[2,256,8192]{2,1,0:T(8,128)(2,1)}, f32[8,2,16,256]{3,2,1,0:T(8,128)}) custom-call(bf16[256,1024]{1,0:T(8,128)(2,1)} %bitcast.11, s32[256,512]{1,0:T(8,128)} %valid_ref.1, s32[16]{0:T(128)} %sel_ref.1), custom_call_target="tpu_custom_call" | custom-call | tf_op jit(solution)/shard_map/pallas_call | solution.py:399
  113.6 0.1 fusion.4
  113.7 2.4 %fusion = f32[16,256,32]{1,2,0:T(8,128)} fusion(f32[8,2,16,256]{3,2,1,0:T(8,128)} %get-tuple-element.5, f32[8,1,32]{2,0,1:T(8,128)S(1)} %get-tuple-element.7, f32[8,1,32]{2,0,1:T(8,128)S(1)} %get-tuple-element.6), kind=kOutput, calls=%fused_computation.1 | convolution fusion | flops 25297408 | bytes 788480 | tf_op jit(solution)/shard_map/frsc,frl->scl/dot_general | solution.py:452
  116.2 7.8 %copy.10 = bf16[1,2,256,8192]{3,2,1,0:T(8,128)(2,1)} copy(bf16[1,2,256,8192]{3,2,1,0:T(8,128)(2,1)} %bitcast.10) | data formatting | bytes 16777216
  (2 shorter events, 0.0 us)

commit v14 on v13

--- a/solution.py
+++ b/solution.py
@@ -329,17 +329,40 @@
     def finish(t):
         zo = (z - step * (t + 1) + 2 * zs) % zs
         part = blk(zo, 1 - xl, c)
-        wait(rows(part, 1 - xl), recv_x.at[1 + t], partner)
-        send(rows(part, 1 - xl), rows(part, 1 - xl), recv_sib.at[2 + 3 * (zs - 1) + t], sib)
-        compute(part)
         zt = (z + step * (t + 1) + 2 * zs) % zs
         sfull = blk(zt, xl, 1 - c)
         spart = blk(zt, 1 - xl, 1 - c)
-        for k, (b, h) in enumerate(((sfull, 0), (sfull, 1), (spart, xl))):
-            wait(rows(b, h), recv_sib.at[2 + 3 * t + k], sib)
-        compute(sfull)
-        wait(rows(spart, 1 - xl), recv_sib.at[2 + 3 * (zs - 1) + t], sib)
-        compute(spart)
+
+        def first():
+            wait(rows(part, 1 - xl), recv_x.at[1 + t], partner)
+            send(rows(part, 1 - xl), rows(part, 1 - xl), recv_sib.at[2 + 3 * (zs - 1) + t], sib)
+            compute(part)
+
+        def second():
+            for k, (b, h) in enumerate(((sfull, 0), (sfull, 1), (spart, xl))):
+                wait(rows(b, h), recv_sib.at[2 + 3 * t + k], sib)
+            compute(sfull)
+
+        def third():
+            wait(rows(spart, 1 - xl), recv_sib.at[2 + 3 * (zs - 1) + t], sib)
+            compute(spart)
+
+        return [first, second, third]
+
+    def sibling_own():
+        wait(held.at[sib], recv_sib.at[0], sib)
+        compute(sib)
+
+    def sibling_across():
+        sib_across = blk(z, 1 - xl, 1 - c)
+        wait(held.at[sib_across], recv_sib.at[1], sib)
+        compute(sib_across)
+
+    pending = []
+
+    def one():
+        if pending:
+            pending.pop(0)()
 
     for s in range(zs - 1):
         zo = (z - step * (s + 1) + 2 * zs) % zs
@@ -351,17 +374,17 @@
             if s < zs - 2:
                 send(rows(b, h), rows(b, h), recv_ring.at[s + 1, k], nxt)
             send(rows(b, h), rows(b, h), recv_sib.at[2 + 3 * s + k], sib)
+            one()
         send(rows(full, xl), rows(full, xl), recv_x.at[1 + s], partner)
-        compute(full)
+        pending.append(functools.partial(compute, full))
         if s == 0:
-            wait(held.at[sib], recv_sib.at[0], sib)
-            compute(sib)
-            sib_across = blk(z, 1 - xl, 1 - c)
-            wait(held.at[sib_across], recv_sib.at[1], sib)
-            compute(sib_across)
+            pending.extend([sibling_own, sibling_across])
         else:
-            finish(s - 1)
-    finish(zs - 2)
+            pending.extend(finish(s - 1))
+        one()
+    pending.extend(finish(zs - 2))
+    while pending:
+        one()
     station = picked[...]
     wide = station.shape[1] // 2
     swapped = jnp.concatenate([station[:, wide:], -station[:, :wide]], axis=1)

time: 124 us -> 125 us (level)
  no operation moved by 1% of the time
where the time goes in v14:
time: 125 us
  Pallas kernels  114 us (91%)
  local copies, waits for them, and re-layouts  7.77 us (6%)
  matrix products  2.43 us (2%)
    pallas_call x1, Pallas kernels, grp_cross(): pl.pallas_call(functools.partial(_cross_kernel, zs, bands, scaling), out_...  114 us
    unnamed x1, local copies, waits for them, and re-layouts  7.77 us

profile of v14, /device:TPU:1, one launch (start us, length us, event | category | flops | bytes accessed | tf_op | source)
XLA Modules:
  0.0 124.8 jit_solution(7856176456784137342)
XLA Ops:
  0.6 113.8 %shard_map.50 = (bf16[2,256,8192]{2,1,0:T(8,128)(2,1)}, f32[8,2,16,256]{3,2,1,0:T(8,128)}) custom-call(bf16[256,1024]{1,0:T(8,128)(2,1)} %bitcast.11, s32[256,512]{1,0:T(8,128)} %valid_ref.1, s32[16]{0:T(128)} %sel_ref.1), custom_call_target="tpu_custom_call" | custom-call | tf_op jit(solution)/shard_map/pallas_call | solution.py:422
  114.4 0.1 fusion.4
  114.5 2.4 %fusion = f32[16,256,32]{1,2,0:T(8,128)} fusion(f32[8,2,16,256]{3,2,1,0:T(8,128)} %get-tuple-element.5, f32[8,1,32]{2,0,1:T(8,128)S(1)} %get-tuple-element.7, f32[8,1,32]{2,0,1:T(8,128)S(1)} %get-tuple-element.6), kind=kOutput, calls=%fused_computation.1 | convolution fusion | flops 25297408 | bytes 788480 | tf_op jit(solution)/shard_map/frsc,frl->scl/dot_general | solution.py:475
  117.0 7.8 %copy.10 = bf16[1,2,256,8192]{3,2,1,0:T(8,128)(2,1)} copy(bf16[1,2,256,8192]{3,2,1,0:T(8,128)(2,1)} %bitcast.10) | data formatting | bytes 16777216
  (2 shorter events, 0.0 us)

commit v15 on v13

--- a/solution.py
+++ b/solution.py
@@ -350,8 +350,9 @@
             wait(rows(b, h), recv_ring.at[s, k], prv)
             if s < zs - 2:
                 send(rows(b, h), rows(b, h), recv_ring.at[s + 1, k], nxt)
+        send(rows(full, xl), rows(full, xl), recv_x.at[1 + s], partner)
+        for k, (b, h) in enumerate(pieces):
             send(rows(b, h), rows(b, h), recv_sib.at[2 + 3 * s + k], sib)
-        send(rows(full, xl), rows(full, xl), recv_x.at[1 + s], partner)
         compute(full)
         if s == 0:
             wait(held.at[sib], recv_sib.at[0], sib)

time: 124 us -> 124 us (level)
  no operation moved by 1% of the time
where the time goes in v15:
time: 124 us
  Pallas kernels  113 us (91%)
  local copies, waits for them, and re-layouts  7.77 us (6%)
  matrix products  2.43 us (2%)
    pallas_call x1, Pallas kernels, grp_cross(): pl.pallas_call(functools.partial(_cross_kernel, zs, bands, scaling), out_...  113 us
    unnamed x1, local copies, waits for them, and re-layouts  7.77 us

profile of v15, /device:TPU:1, one launch (start us, length us, event | category | flops | bytes accessed | tf_op | source)
XLA Modules:
  0.0 123.9 jit_solution(7859371323539248813)
XLA Ops:
  0.6 113.0 %shard_map.50 = (bf16[2,256,8192]{2,1,0:T(8,128)(2,1)}, f32[8,2,16,256]{3,2,1,0:T(8,128)}) custom-call(bf16[256,1024]{1,0:T(8,128)(2,1)} %bitcast.11, s32[256,512]{1,0:T(8,128)} %valid_ref.1, s32[16]{0:T(128)} %sel_ref.1), custom_call_target="tpu_custom_call" | custom-call | tf_op jit(solution)/shard_map/pallas_call | solution.py:400
  113.6 0.1 fusion.4
  113.7 2.4 %fusion = f32[16,256,32]{1,2,0:T(8,128)} fusion(f32[8,2,16,256]{3,2,1,0:T(8,128)} %get-tuple-element.5, f32[8,1,32]{2,0,1:T(8,128)S(1)} %get-tuple-element.7, f32[8,1,32]{2,0,1:T(8,128)S(1)} %get-tuple-element.6), kind=kOutput, calls=%fused_computation.1 | convolution fusion | flops 25297408 | bytes 788480 | tf_op jit(solution)/shard_map/frsc,frl->scl/dot_general | solution.py:453
  116.2 7.8 %copy.10 = bf16[1,2,256,8192]{3,2,1,0:T(8,128)(2,1)} copy(bf16[1,2,256,8192]{3,2,1,0:T(8,128)(2,1)} %bitcast.10) | data formatting | bytes 16777216
  (2 shorter events, 0.0 us)

commit v16 on v15

--- a/solution.py
+++ b/solution.py
@@ -451,7 +451,7 @@
     phase = math.pi * bin_values[:, None] * lag_values[None, :] / LAGS
     lag_table = jnp.stack([jnp.cos(phase), -jnp.sin(phase)], axis=1)
     station_gather = jnp.einsum(
-        "frsc,frl->scl", all_bins, lag_table, precision=lax.Precision.HIGHEST
+        "frsc,frl->scl", all_bins, lag_table, precision=lax.Precision.HIGH
     ) / math.sqrt(total_bins)
     return (cross, station_gather)
 

time: 124 us -> 124 us (level)
  no operation moved by 1% of the time
where the time goes in v16:
time: 124 us
  Pallas kernels  113 us (91%)
  local copies, waits for them, and re-layouts  7.77 us (6%)
  matrix products  2.2 us (2%)
    pallas_call x1, Pallas kernels, grp_cross(): pl.pallas_call(functools.partial(_cross_kernel, zs, bands, scaling), out_...  113 us
    unnamed x1, local copies, waits for them, and re-layouts  7.77 us

profile of v16, /device:TPU:1, one launch (start us, length us, event | category | flops | bytes accessed | tf_op | source)
XLA Modules:
  0.0 123.7 jit_solution(12931653466168323073)
XLA Ops:
  0.6 113.0 %shard_map.50 = (bf16[2,256,8192]{2,1,0:T(8,128)(2,1)}, f32[8,2,16,256]{3,2,1,0:T(8,128)}) custom-call(bf16[256,1024]{1,0:T(8,128)(2,1)} %bitcast.11, s32[256,512]{1,0:T(8,128)} %valid_ref.1, s32[16]{0:T(128)} %sel_ref.1), custom_call_target="tpu_custom_call" | custom-call | tf_op jit(solution)/shard_map/pallas_call | solution.py:400
  113.6 0.1 fusion.4
  113.7 2.2 %fusion = f32[16,256,32]{1,2,0:T(8,128)} fusion(f32[8,2,16,256]{3,2,1,0:T(8,128)} %get-tuple-element.5, f32[8,1,32]{2,0,1:T(8,128)S(1)} %get-tuple-element.7, f32[8,1,32]{2,0,1:T(8,128)S(1)} %get-tuple-element.6), kind=kOutput, calls=%fused_computation.1 | convolution fusion | flops 12714496 | bytes 788480 | tf_op jit(solution)/shard_map/frsc,frl->scl/dot_general | solution.py:453
  115.9 7.8 %copy.10 = bf16[1,2,256,8192]{3,2,1,0:T(8,128)(2,1)} copy(bf16[1,2,256,8192]{3,2,1,0:T(8,128)(2,1)} %bitcast.10) | data formatting | bytes 16777216
  (2 shorter events, 0.0 us)

commit v17 on v15

--- a/solution.py
+++ b/solution.py
@@ -315,14 +315,16 @@
         station_ids = jnp.where(place == k, sel_ref[k], station_ids)
     own = blk(z, xl, c)
     held[own] = x_ref[...]
-    send(x_ref, held.at[own], recv_x.at[0], partner)
+    send(x_ref.at[pl.ds(pl.multiple_of((1 - xl) * half, half), half)], rows(own, 1 - xl), recv_x.at[0], partner)
+    send(x_ref.at[pl.ds(pl.multiple_of(xl * half, half), half)], rows(own, xl), recv_x.at[zs], partner)
     send(x_ref, held.at[own], recv_sib.at[0], sib)
     send(x_ref.at[pl.ds(0, half)], rows(own, 0), recv_ring.at[0, 0], nxt)
     send(x_ref.at[pl.ds(half, half)], rows(own, 1), recv_ring.at[0, 1], nxt)
     compute(own)
     across = blk(z, 1 - xl, c)
-    wait(held.at[across], recv_x.at[0], partner)
+    wait(rows(across, xl), recv_x.at[0], partner)
     send(rows(across, xl), rows(across, xl), recv_ring.at[0, 2], nxt)
+    wait(rows(across, 1 - xl), recv_x.at[zs], partner)
     send(held.at[across], held.at[across], recv_sib.at[1], sib)
     compute(across)
 
@@ -411,7 +413,7 @@
             pltpu.VMEM((selector.shape[0], cols), jnp.float32),
             pltpu.SemaphoreType.DMA((8 * zs + 16,)),
             pltpu.SemaphoreType.DMA((zs - 1, 3)),
-            pltpu.SemaphoreType.DMA((zs,)),
+            pltpu.SemaphoreType.DMA((zs + 1,)),
             pltpu.SemaphoreType.DMA((2 + 4 * (zs - 1),)),
             pltpu.SemaphoreType.DMA((2,)),
             pltpu.SemaphoreType.DMA((bands,)),

time: 124 us -> 123 us (level)
  no operation moved by 1% of the time
where the time goes in v17:
time: 123 us
  Pallas kernels  112 us (91%)
  local copies, waits for them, and re-layouts  7.77 us (6%)
  matrix products  2.43 us (2%)
    pallas_call x1, Pallas kernels, grp_cross(): pl.pallas_call(functools.partial(_cross_kernel, zs, bands, scaling), out_...  112 us
    unnamed x1, local copies, waits for them, and re-layouts  7.77 us

profile of v17, /device:TPU:1, one launch (start us, length us, event | category | flops | bytes accessed | tf_op | source)
XLA Modules:
  0.0 123.0 jit_solution(4666613630187685755)
XLA Ops:
  0.6 112.1 %shard_map.50 = (bf16[2,256,8192]{2,1,0:T(8,128)(2,1)}, f32[8,2,16,256]{3,2,1,0:T(8,128)}) custom-call(bf16[256,1024]{1,0:T(8,128)(2,1)} %bitcast.11, s32[256,512]{1,0:T(8,128)} %valid_ref.1, s32[16]{0:T(128)} %sel_ref.1), custom_call_target="tpu_custom_call" | custom-call | tf_op jit(solution)/shard_map/pallas_call | solution.py:402
  112.7 0.1 fusion.4
  112.8 2.4 %fusion = f32[16,256,32]{1,2,0:T(8,128)} fusion(f32[8,2,16,256]{3,2,1,0:T(8,128)} %get-tuple-element.5, f32[8,1,32]{2,0,1:T(8,128)S(1)} %get-tuple-element.7, f32[8,1,32]{2,0,1:T(8,128)S(1)} %get-tuple-element.6), kind=kOutput, calls=%fused_computation.1 | convolution fusion | flops 25297408 | bytes 788480 | tf_op jit(solution)/shard_map/frsc,frl->scl/dot_general | solution.py:455
  115.3 7.8 %copy.10 = bf16[1,2,256,8192]{3,2,1,0:T(8,128)(2,1)} copy(bf16[1,2,256,8192]{3,2,1,0:T(8,128)(2,1)} %bitcast.10) | data formatting | bytes 16777216
  (2 shorter events, 0.0 us)
